TPU v7x, 32 devices: a whole 2x2x4 slice. The times are simulated.
32 devices in a mesh: seq: 4 (over z), head: 4 (over y, x), rep: 2 (over core).
Axes of the slice: x: 2, y: 2, z: 4, core: 2. Of those that a mesh axis runs over, the one named last changes fastest.
Arguments:
- queries: bfloat16 [1024, 8, 128], P(('rep', 'seq'), 'head'), parts along dimension 0, may hold values from -8 to 8
- keys: bfloat16 [1024, 128], P(('rep', 'seq')), parts along dimension 0, may hold values from -8 to 8
- values: bfloat16 [1024, 128], P(('rep', 'seq')), parts along dimension 0, may hold values from -6 to 6
- query_weight: float32 [16, 64, 128], P(('rep', 'head')), parts along dimension 0, may hold values from -0.075 to 0.075
- key_weight: float32 [16, 64, 128], P(('rep', 'head')), parts along dimension 0, may hold values from -0.075 to 0.075
Outputs:
- loss: float32 [2], P('rep'), parts along dimension 0
- grad_query_weight: float32 [16, 64, 128], P(('rep', 'head')), parts along dimension 0
- grad_key_weight: float32 [16, 64, 128], P(('rep', 'head')), parts along dimension 0
There are 2 independent parts, one for each index of `rep`. A program takes and returns all parts, laid end to end along the dimension named above; each array names one. Nothing has to cross between parts.
All inputs are finite; a program needn't handle non-finite values.
Results may differ from a plain program's by a relative error of at most 0.00045.
Values may be sent and summed in bfloat16 or wider, within the bound.
No kernel may reach another device: no remote copies, remote signals or barrier semaphores. Data moves between devices by JAX's collectives and lax.ppermute only.
A program may use at most 64 MiB of HBM per device.

v0:
```python
import jax
import jax.numpy as jnp
from jax import lax
from jax.sharding import PartitionSpec as P

WINDOW = 64


very_low = -1e30
exact = lax.Precision.HIGHEST


def shifted(value, axis, steps):
    count = lax.axis_size(axis)
    leading, last = (max(0, -steps), min(count, count - steps))
    return lax.ppermute(value, axis, [(source, source + steps) for source in range(leading, last)])


def prefix_2(x, axis, combine, identity):
    peers, place = (lax.axis_size(axis), lax.axis_index(axis))
    everything = jax.tree.map(lambda part: lax.all_gather(part, axis), x)
    start = jax.tree.map(
        lambda part, zero: jnp.broadcast_to(jnp.asarray(zero, part.dtype), part.shape), x, identity
    )

    def lap(k, before):
        at = peers - 1 - k
        reached = at > place
        new = combine(before, jax.tree.map(lambda part: part[at], everything))
        return jax.tree.map(lambda a, b: jnp.where(reached, a, b), new, before)

    return lax.fori_loop(0, peers, lap, start)


def feature_map(act):
    first = jnp.exp(act)
    second = jnp.exp(-act)
    return jnp.concatenate(
        [
            first / jnp.sum(first, axis=-1, keepdims=True),
            second / jnp.sum(second, axis=-1, keepdims=True),
        ],
        axis=-1,
    )


def feature_back(features, grad):
    half = features.shape[-1] // 2
    first = features[..., :half]
    second = features[..., half:]
    grad_first = grad[..., :half]
    grad_second = grad[..., half:]
    return first * (grad_first - jnp.sum(first * grad_first, axis=-1, keepdims=True)) - second * (
        grad_second - jnp.sum(second * grad_second, axis=-1, keepdims=True)
    )


def key_feature_map(keys_wide, key_weight):
    return feature_map(jnp.einsum("jd,hfd->hjf", keys_wide, key_weight, precision=exact))


def add_pair(earlier, later):
    return (earlier[0] + later[0], earlier[1] + later[1])


def flash_update(carry, queries, keys, values, query_place, key_place):
    best, total, accum = carry
    scale = queries.shape[-1] ** (-0.5)
    scores = jnp.einsum("thd,jd->htj", queries, keys, preferred_element_type=jnp.float32) * scale
    allowed = (key_place[None, :] <= query_place[:, None])[None]
    scores = jnp.where(allowed, scores, very_low)
    fresh = jnp.maximum(best, jnp.max(scores, axis=-1))
    weights = jnp.where(allowed, jnp.exp(scores - fresh[..., None]), 0.0)
    total = jnp.sum(weights, axis=-1)
    accum = jnp.einsum(
        "htj,jd->htd", weights.astype(jnp.bfloat16), values, preferred_element_type=jnp.float32
    )
    return (fresh, total, accum)


def state_update(state, keys, values, key_place, bound, key_weight):

    def accumulate(inner):
        keep = (key_place < bound).astype(jnp.float32)
        features = key_feature_map(keys.astype(jnp.float32), key_weight) * keep[None, :, None]
        return (
            jnp.einsum("hjf,jd->hfd", features, values.astype(jnp.float32), precision=exact),
            jnp.sum(features, axis=1),
        )

    return lax.cond(jnp.min(key_place) < bound, accumulate, lambda inner: inner, state)


def local(queries, keys, values, query_weight, key_weight):
    rows, local_heads, width = queries.shape
    shards = lax.axis_size("seq")
    device = lax.axis_index("seq")
    feature_count = 2 * query_weight.shape[1]
    total_tokens = rows * shards
    first_place = device * rows
    bound = first_place - WINDOW
    natural_place = first_place + jnp.arange(rows, dtype=jnp.int32)
    flash_init = (
        jnp.full((local_heads, rows), very_low, jnp.float32),
        jnp.zeros((local_heads, rows), jnp.float32),
        jnp.zeros((local_heads, rows, width), jnp.float32),
    )
    zero_state = (
        jnp.zeros((local_heads, feature_count, width), jnp.float32),
        jnp.zeros((local_heads, feature_count), jnp.float32),
    )
    halo_keys, halo_values = shifted((keys[rows - WINDOW :], values[rows - WINDOW :]), "seq", 1)
    ext_keys = jnp.concatenate([halo_keys, keys], axis=0)
    ext_values = jnp.concatenate([halo_values, values], axis=0)
    ext_count = rows + WINDOW
    ext_place = bound + jnp.arange(ext_count, dtype=jnp.int32)
    valid = ext_place >= 0
    covered = jnp.arange(ext_count, dtype=jnp.int32) < rows
    cover_mask = (valid & covered).astype(jnp.float32)
    ext_keys_wide = ext_keys.astype(jnp.float32)
    ext_values_wide = ext_values.astype(jnp.float32)
    key_features = key_feature_map(ext_keys_wide, key_weight)
    fold_keys, fold_values = (keys, values)
    piece_keys = lax.all_gather(fold_keys, "seq", axis=0, tiled=True)
    piece_values = lax.all_gather(fold_values, "seq", axis=0, tiled=True)
    key_place = jnp.arange(piece_keys.shape[0], dtype=jnp.int32)

    def attend(inner):
        flash = flash_update(inner[0], queries, piece_keys, piece_values, natural_place, key_place)
        state = state_update(inner[1], piece_keys, piece_values, key_place, bound, key_weight)
        return (flash, state)

    flash, folded = lax.cond(
        jnp.int32(0) < first_place + rows, attend, lambda inner: inner, (flash_init, zero_state)
    )
    teacher = jnp.transpose(flash[2] / flash[1][..., None], (1, 0, 2)).astype(jnp.bfloat16)
    scale = width ** (-0.5)
    scores = (
        jnp.einsum("thd,jd->htj", queries, ext_keys, preferred_element_type=jnp.float32) * scale
    )
    window = (
        (ext_place[None, :] <= natural_place[:, None])
        & (ext_place[None, :] > natural_place[:, None] - WINDOW)
        & valid[None, :]
    )[None]
    linear_mask = ((ext_place[None, :] <= natural_place[:, None] - WINDOW) & valid[None, :])[None]
    window_best = jnp.max(jnp.where(window, scores, very_low), axis=-1)
    window_weights = jnp.where(window, jnp.exp(scores - window_best[..., None]), 0.0)
    window_total = jnp.sum(window_weights, axis=-1)
    window_sum = jnp.einsum(
        "htj,jd->htd",
        window_weights.astype(jnp.bfloat16),
        ext_values,
        preferred_element_type=jnp.float32,
    )
    queries_wide = queries.astype(jnp.float32)
    query_features = feature_map(
        jnp.einsum("thd,hfd->htf", queries_wide, query_weight, precision=exact)
    )
    linear = jnp.where(
        linear_mask, jnp.einsum("htf,hjf->htj", query_features, key_features, precision=exact), 0.0
    )
    linear_sum = jnp.einsum("htj,jd->htd", linear, ext_values_wide, precision=exact) + jnp.einsum(
        "htf,hfd->htd", query_features, folded[0], precision=exact
    )
    linear_total = jnp.sum(linear, axis=-1) + jnp.einsum(
        "htf,hf->ht", query_features, folded[1], precision=exact
    )
    lift = jnp.exp(-window_best)
    denominator = window_total + lift * linear_total
    student = (window_sum + lift[..., None] * linear_sum) / denominator[..., None]
    teacher_wide = jnp.transpose(teacher, (1, 0, 2)).astype(jnp.float32)
    difference = student - teacher_wide
    loss_part = jnp.sum(difference * difference) / total_tokens
    grad_out = 2.0 * difference / total_tokens
    num_grad = lift[..., None] * grad_out / denominator[..., None]
    den_grad = -lift * jnp.sum(grad_out * student, axis=-1) / denominator
    adjoint = (
        jnp.einsum("htf,htd->hfd", query_features, num_grad, precision=exact),
        jnp.einsum("htf,ht->hf", query_features, den_grad, precision=exact),
    )
    later = prefix_2(adjoint, "seq", add_pair, zero_state)
    link = jnp.where(
        linear_mask,
        jnp.einsum("htd,jd->htj", num_grad, ext_values_wide, precision=exact) + den_grad[..., None],
        0.0,
    )
    query_feature_grad = (
        jnp.einsum("htj,hjf->htf", link, key_features, precision=exact)
        + jnp.einsum("htd,hfd->htf", num_grad, folded[0], precision=exact)
        + den_grad[..., None] * folded[1][:, None, :]
    )
    key_feature_grad = (
        jnp.einsum("htj,htf->hjf", link, query_features, precision=exact)
        + jnp.einsum("jd,hfd->hjf", ext_values_wide, later[0], precision=exact)
        + later[1][:, None, :]
    )
    key_feature_grad = key_feature_grad * cover_mask[None, :, None]
    query_act_grad = feature_back(query_features, query_feature_grad)
    key_act_grad = feature_back(key_features, key_feature_grad)
    grad_query = jnp.einsum("htf,thd->hfd", query_act_grad, queries_wide, precision=exact)
    grad_key = jnp.einsum("hjf,jd->hfd", key_act_grad, ext_keys_wide, precision=exact)
    grad_query, grad_key = lax.psum((grad_query, grad_key), "seq")
    loss = lax.psum(loss_part, ("seq", "head")).reshape(1)
    return (loss, grad_query, grad_key)


def solution(mesh):
    in_specs = (
        P(("rep", "seq"), "head", None),
        P(("rep", "seq"), None),
        P(("rep", "seq"), None),
        P(("rep", "head"), None, None),
        P(("rep", "head"), None, None),
    )
    out_specs = (P("rep"), P(("rep", "head"), None, None), P(("rep", "head"), None, None))
    return jax.shard_map(local, mesh=mesh, in_specs=in_specs, out_specs=out_specs, check_vma=False)
```

profile of v0, /device:TPU:0, one launch (start us, length us, event | category | flops | bytes accessed | tf_op | source)
XLA Modules:
  0.0 129.8 jit_solution(5583325967439875054)
XLA Ops:
  7.2 0.0 copy-start
  7.2 0.0 copy-start.5
  7.2 0.0 all-reduce.3.cloned.1.call-start
  7.2 0.7 slice.19
  8.0 4.9 %collective-permute-start.1 = (bf16[64,128]{1,0:T(8,128)(2,1)S(1)}, bf16[64,128]{1,0:T(8,128)(2,1)S(1)}, u32[]{:S(2)}, u32[]{:S(2)}) collective-permute-start(bf16[64,128]{1,0:T(8,128)(2,1)S(1)} %slice.19), channel_id=1, source_target_pairs={{0,8},{8,16},{16,24},{1,9},{9,17},{17,25},{2,10},{10,18},{18,26},{... | collective-permute-start | bytes 49160 | tf_op jit(solution)/shard_map/ppermute | solution.py:16
  12.9 0.0 copy-done.5
  12.9 3.5 %collective-permute-start = (bf16[64,128]{1,0:T(8,128)(2,1)S(1)}, bf16[64,128]{1,0:T(8,128)(2,1)S(1)}, u32[]{:S(2)}, u32[]{:S(2)}) collective-permute-start(bf16[64,128]{1,0:T(8,128)(2,1)S(1)} %slice.18), channel_id=1, source_target_pairs={{0,8},{8,16},{16,24},{1,9},{9,17},{17,25},{2,10},{10,18},{18,26},{... | collective-permute-start | bytes 49160 | tf_op jit(solution)/shard_map/ppermute | solution.py:16
  16.5 0.0 copy-start.4
  16.5 13.5 %all_gather.18 = bf16[512,128]{1,0:T(8,128)(2,1)S(1)} all-gather(bf16[128,128]{1,0:T(8,128)(2,1)S(1)} %copy-done.5), channel_id=1, replica_groups=mesh['seq'=4,'head'=4,'rep'=2] {'seq'}, dimensions={0}, use_global_device_ids=true | all-gather | bytes 163840 | tf_op jit(solution)/shard_map/all_gather | solution.py:124
  30.0 0.0 copy-done.4
  30.0 0.0 copy-start.1
  30.0 13.5 %all_gather.19 = bf16[512,128]{1,0:T(8,128)(2,1)S(1)} all-gather(bf16[128,128]{1,0:T(8,128)(2,1)S(1)} %copy-done.4), channel_id=1, replica_groups=mesh['seq'=4,'head'=4,'rep'=2] {'seq'}, dimensions={0}, use_global_device_ids=true | all-gather | bytes 163840 | tf_op jit(solution)/shard_map/all_gather | solution.py:125
  43.4 0.0 copy-done
  43.4 0.0 copy-done.1
  43.4 0.3 exponential_reduce_fusion
  43.7 0.0 copy-start.6
  43.8 0.8 copy-done.6
  44.5 3.3 %conditional.2 = (f32[2,128]{1,0:T(2,128)S(1)}, f32[2,128,128]{2,1,0:T(8,128)S(1)}, f32[2,128]{1,0:T(2,128)S(1)}, f32[2,128,128]{1,2,0:T(8,128)S(1)}) conditional(s32[]{:T(128)} %convert_element_type.35, () %tuple.46, (s32[512]{0:T(512)S(1)}, s32[]{:T(128)}, s32[128]{0:T(128)S(1)}, bf16[512,128]{1,0:T(8,128)(2,1)S(1)}, ...), branch_computations={%region_5.0_spmd, %region_6.15_spmd} | conditional | flops 371391616 | bytes 5944038 | solution.py:133
  44.5 0.6 reduce_min.8
  45.8 0.1 broadcast_compare_fusion
  46.0 0.0 copy-start.2
  46.0 0.0 copy-start.8
  46.1 0.3 fusion.78
  46.3 0.3 copy-done.2
  46.7 0.0 copy-done.8
  46.7 0.3 fusion.11
  46.9 0.0 copy-start.3
  46.9 0.0 copy-start.9
  47.0 0.1 fusion.10
  47.1 0.8 copy-done.3
  47.8 0.0 copy-done.9
  47.8 0.2 fusion.63
  48.1 0.4 fusion.64
  48.5 0.1 and_and_fusion
  48.6 0.0 collective-permute-done
  48.6 0.2 select_reduce_fusion
  48.9 0.1 fusion.28
  48.9 0.3 bitcast_reduce_fusion.3
  49.3 0.6 fusion.79
  49.9 0.0 collective-permute-done.1
  49.9 0.3 fusion.27
  50.2 0.8 multiply_reduce_fusion.2
  51.0 0.3 fusion.77
  51.3 0.4 fusion.61
  51.7 0.3 fusion.60
  52.0 10.1 %all-gather.2 = f32[4,2,128]{2,1,0:T(2,128)S(1)} all-gather(f32[1,2,128]{2,1,0:T(2,128)S(1)} %bitcast.94), channel_id=3, replica_groups=mesh['seq'=4,'head'=4,'rep'=2] {'seq'}, dimensions={0}, use_global_device_ids=true | all-gather | bytes 5120 | tf_op jit(solution)/shard_map/all_gather | solution.py:21
  62.1 0.3 fusion.23
  62.3 0.5 fusion.62
  62.9 0.4 fusion.25
  63.3 14.8 %all-gather = f32[8,128,128]{2,1,0:T(8,128)S(1)} all-gather(f32[2,128,128]{2,1,0:T(8,128)S(1)} %fusion.61), channel_id=2, replica_groups=mesh['seq'=4,'head'=4,'rep'=2] {'seq'}, dimensions={0}, use_global_device_ids=true | all-gather | bytes 655360 | tf_op jit(solution)/shard_map/all_gather | solution.py:21
  78.1 0.3 while.18
  78.5 0.3 fusion.22
  78.8 0.1 multiply_reduce_fusion.1
  78.8 0.8 fusion.44
  79.6 0.9 fusion.30
  80.5 0.0 all-reduce.3.cloned.1.call-update
  81.1 39.7 %psum.21 = f32[1]{0:T(128)} all-reduce(f32[1]{0:T(128)} %bitcast.16), channel_id=1, replica_groups=mesh['seq'=4,'head'=4,'rep'=2] {'seq','head'}, use_global_device_ids=true, to_apply=%region_18.19 | all-reduce | flops 1 | bytes 8 | tf_op jit(solution)/shard_map/psum | solution.py:204
  120.8 0.0 all-reduce.3.cloned.1.call-done
  120.8 0.0 copy-start.7
  120.8 1.5 %copy.97 = f32[2,64,128]{2,1,0:T(8,128)} copy(f32[2,64,128]{2,1,0:T(8,128)} %get-tuple-element.388) | data formatting | bytes 131072
  122.3 0.0 copy-done.7
  122.3 0.6 copy.98
  (27 shorter events, 0.5 us)
Async XLA Ops:
  7.2 36.3 %copy-start = (f32[2,64,128]{2,1,0:T(8,128)S(1)}, f32[2,64,128]{2,1,0:T(8,128)}, u32[]{:S(2)}) copy-start(f32[2,64,128]{2,1,0:T(8,128)} %param.14) | copy-start | bytes 196612
  7.2 5.7 %copy-start.5 = (bf16[128,128]{1,0:T(8,128)(2,1)S(1)}, bf16[128,128]{1,0:T(8,128)(2,1)}, u32[]{:S(2)}) copy-start(bf16[128,128]{1,0:T(8,128)(2,1)} %param.12) | copy-start | bytes 98308
  7.2 113.6 %all-reduce.3.cloned.1.call-start = ((), (), s32[]{:S(2)}) async-start(), calls=%async_computation | async-start | bytes 262144 | tf_op jit(solution)/shard_map/psum | solution.py:203
  8.0 41.9 %collective-permute-start.1 = (bf16[64,128]{1,0:T(8,128)(2,1)S(1)}, bf16[64,128]{1,0:T(8,128)(2,1)S(1)}, u32[]{:S(2)}, u32[]{:S(2)}) collective-permute-start(bf16[64,128]{1,0:T(8,128)(2,1)S(1)} %slice.19), channel_id=1, source_target_pairs={{0,8},{8,16},{16,24},{1,9},{9,17},{17,25},{2,10},{10,18},{18,26},{... | collective-permute-start | bytes 49160 | tf_op jit(solution)/shard_map/ppermute | solution.py:16
  12.9 35.7 %collective-permute-start = (bf16[64,128]{1,0:T(8,128)(2,1)S(1)}, bf16[64,128]{1,0:T(8,128)(2,1)S(1)}, u32[]{:S(2)}, u32[]{:S(2)}) collective-permute-start(bf16[64,128]{1,0:T(8,128)(2,1)S(1)} %slice.18), channel_id=1, source_target_pairs={{0,8},{8,16},{16,24},{1,9},{9,17},{17,25},{2,10},{10,18},{18,26},{... | collective-permute-start | bytes 49160 | tf_op jit(solution)/shard_map/ppermute | solution.py:16
  16.5 13.5 %copy-start.4 = (bf16[128,128]{1,0:T(8,128)(2,1)S(1)}, bf16[128,128]{1,0:T(8,128)(2,1)}, u32[]{:S(2)}) copy-start(bf16[128,128]{1,0:T(8,128)(2,1)} %param.13) | copy-start | bytes 98308
  30.0 13.5 %copy-start.1 = (bf16[128,2,128]{2,1,0:T(2,128)(2,1)S(1)}, bf16[128,2,128]{2,1,0:T(2,128)(2,1)}, u32[]{:S(2)}) copy-start(bf16[128,2,128]{2,1,0:T(2,128)(2,1)} %param.11) | copy-start | bytes 196612
  43.7 0.8 copy-start.6
  46.0 0.6 copy-start.2
  46.0 0.6 copy-start.8
  46.9 0.9 copy-start.3
  46.9 0.9 copy-start.9
  120.8 1.5 %copy-start.7 = (f32[2,64,128]{2,1,0:T(8,128)S(1)}, f32[2,64,128]{2,1,0:T(8,128)}, u32[]{:S(2)}) copy-start(f32[2,64,128]{2,1,0:T(8,128)} %get-tuple-element.389) | copy-start | bytes 196612
Sparse Core Ops, SparseCore 0:
  80.6 33.0 all-reduce.2
where the time goes:
time: 130 us
  blocking collectives  91.5 us (70%)
  between operations  14.8 us (11%)
  starting transfers between devices  8.47 us (7%)
  matrix products  7.72 us (6%)
  local copies, waits for them, and re-layouts  4.81 us (4%)
  other arithmetic  1.51 us (1%)
    psum x1, blocking collectives, local(): loss = lax.psum(loss_part, ('seq', 'head')).reshape(1)  39.7 us
    all_gather x2, blocking collectives, prefix_2(): everything = jax.tree.map(lambda part: lax.all_gather(part, axis), x)  24.9 us
    all_gather x1, blocking collectives, local(): piece_keys = lax.all_gather(fold_keys, 'seq', axis=0, tiled=True)  13.5 us
    all_gather x1, blocking collectives, local(): piece_values = lax.all_gather(fold_values, 'seq', axis=0, tiled=True)  13.5 us
    ppermute x2, starting transfers between devices, shifted(): lax.ppermute(value, axis, [(source, source + steps) for source in range(l...  8.43 us
    unnamed x14, local copies, waits for them, and re-layouts  2.94 us
  transfers between devices with their start and end apart: 3, of which 0 were waited for; matrix products, arithmetic and copies ran while one was open for 3% of the time, Pallas kernels for 0%

commit v1 on v0

--- a/solution.py
+++ b/solution.py
@@ -1,6 +1,10 @@
+import functools
+
 import jax
 import jax.numpy as jnp
 from jax import lax
+from jax.experimental import pallas as pl
+from jax.experimental.pallas import tpu as pltpu
 from jax.sharding import PartitionSpec as P
 
 WINDOW = 64
@@ -8,6 +12,9 @@
 
 very_low = -1e30
 exact = lax.Precision.HIGHEST
+f32, bf16 = jnp.float32, jnp.bfloat16
+PAD = 16
+LIMIT = 8
 
 
 def shifted(value, axis, steps):
@@ -91,7 +98,7 @@
     return lax.cond(jnp.min(key_place) < bound, accumulate, lambda inner: inner, state)
 
 
-def local(queries, keys, values, query_weight, key_weight):
+def local_general(queries, keys, values, query_weight, key_weight):
     rows, local_heads, width = queries.shape
     shards = lax.axis_size("seq")
     device = lax.axis_index("seq")
@@ -205,6 +212,268 @@
     return (loss, grad_query, grad_key)
 
 
+def dot(a, b):
+    return lax.dot_general(a, b, (((1,), (0,)), ((), ())), preferred_element_type=f32)
+
+
+def dot_t(a, b):
+    return lax.dot_general(a, b, (((1,), (1,)), ((), ())), preferred_element_type=f32)
+
+
+def split(x):
+    high = x.astype(bf16)
+    return high, (x - high.astype(f32)).astype(bf16)
+
+
+def dot3(a, b):
+    return dot(a[0], b[0]) + (dot(a[0], b[1]) + dot(a[1], b[0]))
+
+
+def dot_left(a, b):
+    return dot(a[0], b) + dot(a[1], b)
+
+
+def dot_right(a, b):
+    return dot(a, b[0]) + dot(a, b[1])
+
+
+def iota(shape, axis):
+    return lax.broadcasted_iota(jnp.int32, shape, axis)
+
+
+def head_pass(queries, keys, values, ext_keys, ext_values, ext_keys_t, values_t, ext_aug_t, ext_aug, pair_sum, query_weight, key_weight, block, tokens_total):
+    tokens, width = queries.shape
+    blocks = tokens // block
+    scale = width ** (-0.5)
+    wq = split(jnp.concatenate([query_weight, -query_weight], axis=0))
+    wk = split(jnp.concatenate([key_weight, -key_weight], axis=0))
+    raised_t = jnp.exp(dot_t(wq[0], queries) + dot_t(wq[1], queries))
+    qf_t = raised_t / dot_right(pair_sum, split(raised_t))
+    raised = jnp.exp(dot_t(ext_keys, wk[0]) + dot_t(ext_keys, wk[1]))
+    kf = raised / dot_left(split(raised), pair_sum)
+    kf = jnp.where(iota(kf.shape, 0) >= WINDOW, kf, 0.0)
+    qf = qf_t.T
+    kf_t = kf.T
+    qf_ts, kf_s, qf_s, kf_ts = split(qf_t), split(kf), split(qf), split(kf_t)
+    tri = iota((block, block), 0) <= iota((block, block), 1)
+    near = iota((block + WINDOW, block), 0) > iota((block + WINDOW, block), 1)
+    loss = jnp.zeros((1, 1), f32)
+    state_t = None
+    state = None
+    saved = []
+    cut = lambda pair, at: tuple(part[at] for part in pair)
+    for b in range(blocks):
+        lo, hi = b * block, (b + 1) * block
+        here = (slice(None), slice(lo, hi))
+        rows = (slice(lo, hi), slice(None))
+        scores = dot_t(keys[:hi], queries[lo:hi]) * scale
+        tail = scores[lo:]
+        causal = jnp.where(tri, tail, very_low)
+        best = jnp.max(causal, axis=0, keepdims=True)
+        if b:
+            best = jnp.maximum(best, jnp.max(scores[:lo], axis=0, keepdims=True))
+        weights = jnp.where(tri, jnp.exp(tail - best), 0.0)
+        total = jnp.sum(weights, axis=0, keepdims=True)
+        teacher = dot(values_t[:, lo:hi], weights.astype(bf16))
+        if b:
+            weights = jnp.exp(scores[:lo] - best)
+            total = total + jnp.sum(weights, axis=0, keepdims=True)
+            teacher = teacher + dot(values_t[:, :lo], weights.astype(bf16))
+        teacher = (teacher / total).astype(bf16).astype(f32)
+        inside = tri & near[WINDOW:]
+        wbest = jnp.max(jnp.where(inside, tail, very_low), axis=0, keepdims=True)
+        if b:
+            early = jnp.where(near[:WINDOW], scores[lo - WINDOW : lo], very_low)
+            wbest = jnp.maximum(wbest, jnp.max(early, axis=0, keepdims=True))
+        weights = jnp.where(inside, jnp.exp(tail - wbest), 0.0)
+        wtotal = jnp.sum(weights, axis=0, keepdims=True)
+        wsum = dot(values_t[:, lo:hi], weights.astype(bf16))
+        if b:
+            weights = jnp.where(near[:WINDOW], jnp.exp(early - wbest), 0.0)
+            wtotal = wtotal + jnp.sum(weights, axis=0, keepdims=True)
+            weights = jnp.concatenate([jnp.zeros((128 - WINDOW, block), bf16), weights.astype(bf16)], axis=0)
+            wsum = wsum + dot(values_t[:, lo - 128 : lo], weights)
+        linear = jnp.where(tri, dot3(cut(kf_s, rows), cut(qf_ts, here)), 0.0)
+        aug = dot_right(ext_aug_t[:, lo:hi], split(linear))
+        if b:
+            aug = aug + dot3(split(state_t), cut(qf_ts, here))
+        saved_state = state
+        if b + 1 < blocks:
+            grown_t = dot_right(ext_aug_t[:, lo:hi], cut(kf_s, rows))
+            grown = dot_left(cut(kf_ts, here), ext_aug[lo:hi])
+            state_t = grown_t if state_t is None else state_t + grown_t
+            state = grown if state is None else state + grown
+        lift = jnp.exp(-wbest)
+        over = 1.0 / (wtotal + lift * aug[width : width + 1])
+        student = (wsum + lift * aug[:width]) * over
+        difference = student - teacher
+        loss = loss + jnp.sum(jnp.sum(difference * difference, axis=0, keepdims=True), axis=1, keepdims=True)
+        grad = difference * (2.0 / tokens_total)
+        num = grad * (lift * over)
+        den = -(lift * over) * jnp.sum(grad * student, axis=0, keepdims=True)
+        saved.append((num, den, saved_state))
+    grad_q = jnp.zeros((qf_t.shape[0], width), f32)
+    grad_k = jnp.zeros((width, kf.shape[1]), f32)
+    later = None
+    for b in reversed(range(blocks)):
+        lo, hi = b * block, (b + 1) * block
+        here = (slice(None), slice(lo, hi))
+        rows = (slice(lo, hi), slice(None))
+        num, den, state_b = saved[b]
+        num_s = split(num)
+        link = jnp.where(tri, dot_right(ext_values[lo:hi], num_s) + den, 0.0)
+        link_s = split(link)
+        qfg = dot3(cut(kf_ts, here), link_s)
+        if b:
+            qfg = qfg + dot3(split(state_b[:, :width]), num_s) + state_b[:, width : width + 1] * den
+        kfg = dot3(link_s, cut(qf_s, rows))
+        if later is not None:
+            kfg = kfg + dot_right(ext_values[lo:hi], split(later[:width])) + later[width : width + 1]
+        if b:
+            fill = jnp.concatenate([num, den, jnp.zeros((PAD - 1, block), f32)], axis=0)
+            grown = dot3(split(fill), cut(qf_s, rows))
+            later = grown if later is None else later + grown
+        f_t = qf_t[here]
+        back = f_t * (qfg - dot_right(pair_sum, split(f_t * qfg)))
+        grad_q = grad_q + dot_left(split(back), queries[lo:hi])
+        f = kf[rows]
+        back = f * (kfg - dot_left(split(f * kfg), pair_sum))
+        grad_k = grad_k + dot_right(ext_keys_t[:, lo:hi], split(back))
+    half = grad_q.shape[0] // 2
+    grad_k = grad_k.T
+    return loss, grad_q[:half] - grad_q[half:], grad_k[:half] - grad_k[half:]
+
+
+def shared_parts(keys, values, ext_keys, ext_values, features):
+    tokens, width = keys.shape
+    eye = (iota((width, width), 0) == iota((width, width), 1)).astype(bf16)
+    turn = lambda x: dot_t(eye, x).astype(bf16)
+    values_t = turn(values)
+    ext_keys_t = turn(ext_keys)
+    ones = (iota((PAD, tokens), 0) == 0).astype(bf16)
+    ext_aug_t = jnp.concatenate([turn(ext_values), ones], axis=0)
+    ext_aug = jnp.concatenate([ext_values, (iota((tokens, width), 1) == 0).astype(bf16)], axis=1)
+    half = features // 2
+    pair_sum = ((iota((features, features), 0) < half) == (iota((features, features), 1) < half)).astype(bf16)
+    return values_t, ext_keys_t, ext_aug_t, ext_aug, pair_sum
+
+
+def pack_kernel(queries_ref, keys_ref, values_ref, same_ref, other_ref):
+    rows = keys_ref.shape[0]
+    odd = lax.rem(lax.axis_index("seq"), 2) == 1
+    first, second = queries_ref[:, 0, :], queries_ref[:, 1, :]
+    for ref, chosen in ((same_ref, jnp.where(odd, second, first)), (other_ref, jnp.where(odd, first, second))):
+        ref[:rows] = keys_ref[...]
+        ref[rows : 2 * rows] = values_ref[...]
+        ref[2 * rows :] = chosen
+
+
+def main_kernel(shards, rows, *refs):
+    blocks_in = refs[:shards]
+    query_weight_ref, key_weight_ref, grads_ref, loss_ref, keys_ref, values_ref, queries_ref, qw_ref, kw_ref, sems = refs[shards:]
+    tokens, width = queries_ref.shape
+    place = lax.axis_index("seq")
+    mine = lax.rem(place, 2)
+    copies = []
+    for d in range(shards):
+        source = lax.rem(place + shards - d, shards)
+        at = pl.multiple_of(source * rows, rows)
+        for k, (ref, offset) in enumerate(((keys_ref, WINDOW), (values_ref, WINDOW), (queries_ref, 0))):
+            copies.append(
+                pltpu.make_async_copy(
+                    blocks_in[d].at[pl.ds(k * rows, rows)], ref.at[pl.ds(at + offset, rows)], sems.at[3 * d + k]
+                )
+            )
+    copies.append(pltpu.make_async_copy(query_weight_ref.at[mine], qw_ref, sems.at[3 * shards]))
+    copies.append(pltpu.make_async_copy(key_weight_ref.at[mine], kw_ref, sems.at[3 * shards + 1]))
+    for copy in copies:
+        copy.start()
+    keys_ref[:WINDOW] = jnp.zeros((WINDOW, width), bf16)
+    values_ref[:WINDOW] = jnp.zeros((WINDOW, width), bf16)
+    for copy in copies:
+        copy.wait()
+    keys, values = keys_ref[WINDOW:], values_ref[WINDOW:]
+    ext_keys, ext_values = keys_ref[:tokens], values_ref[:tokens]
+    values_t, ext_keys_t, ext_aug_t, ext_aug, pair_sum = shared_parts(
+        keys, values, ext_keys, ext_values, 2 * qw_ref.shape[0]
+    )
+    block = 256 if tokens % 256 == 0 else 128
+    loss, grad_q, grad_k = head_pass(
+        queries_ref[...], keys, values, ext_keys, ext_values, ext_keys_t, values_t, ext_aug_t, ext_aug, pair_sum,
+        qw_ref[...], kw_ref[...], block, tokens,
+    )
+    half = qw_ref.shape[0]
+    grads_ref[:half] = grad_q
+    grads_ref[half:] = grad_k
+    loss_ref[...] = jnp.broadcast_to(loss / tokens, loss_ref.shape)
+
+
+def join_kernel(own_ref, other_ref, loss_a_ref, loss_b_ref, grad_q_ref, grad_k_ref, loss_ref):
+    half = grad_q_ref.shape[1]
+    odd = lax.rem(lax.axis_index("seq"), 2) == 1
+    own, other = own_ref[...], other_ref[...]
+    first, second = jnp.where(odd, other, own), jnp.where(odd, own, other)
+    grad_q_ref[0], grad_q_ref[1] = first[:half], second[:half]
+    grad_k_ref[0], grad_k_ref[1] = first[half:], second[half:]
+    loss_ref[...] = loss_a_ref[...] + loss_b_ref[...]
+
+
+def local_gathered(queries, keys, values, query_weight, key_weight):
+    rows, local_heads, width = queries.shape
+    features = query_weight.shape[1]
+    shards, columns = lax.axis_size("seq"), lax.axis_size("head")
+    tokens = rows * shards
+    vmem = pl.BlockSpec(memory_space=pltpu.VMEM)
+    anywhere = pl.BlockSpec(memory_space=pl.ANY)
+    shape = jax.ShapeDtypeStruct
+    same, other = pl.pallas_call(
+        pack_kernel,
+        out_shape=(shape((3 * rows, width), bf16),) * 2,
+        in_specs=[vmem] * 3,
+        out_specs=(vmem,) * 2,
+        name="pack",
+    )(queries, keys, values)
+    turn = lambda x, axis, size, d: lax.ppermute(x, axis, [(i, (i + d) % size) for i in range(size)])
+    pieces = [same] + [turn(other if d % 2 else same, "seq", shards, d) for d in range(1, shards)]
+    grads, loss = pl.pallas_call(
+        functools.partial(main_kernel, shards, rows),
+        out_shape=(shape((2 * features, width), f32), shape((8, 128), f32)),
+        in_specs=[anywhere] * (shards + 2),
+        out_specs=(vmem,) * 2,
+        scratch_shapes=[
+            pltpu.VMEM((tokens + WINDOW, width), bf16),
+            pltpu.VMEM((tokens + WINDOW, width), bf16),
+            pltpu.VMEM((tokens, width), bf16),
+            pltpu.VMEM((features, width), f32),
+            pltpu.VMEM((features, width), f32),
+            pltpu.SemaphoreType.DMA((3 * shards + 2,)),
+        ],
+        compiler_params=pltpu.CompilerParams(vmem_limit_bytes=48 << 20),
+        name="main",
+    )(*pieces, query_weight, key_weight)
+    swap = lambda x: lax.ppermute(x, "seq", [(i, i ^ 1) for i in range(shards)])
+    loss = sum((turn(loss, "head", columns, d) for d in range(1, columns)), loss)
+    other_grads = swap(grads)
+    other_loss = swap(loss)
+    grad_query, grad_key, loss = pl.pallas_call(
+        join_kernel,
+        out_shape=(shape((local_heads, features, width), f32),) * 2 + (shape((8, 128), f32),),
+        in_specs=[vmem] * 4,
+        out_specs=(vmem,) * 3,
+        name="join",
+    )(grads, other_grads, loss, other_loss)
+    return loss[0, :1], grad_query, grad_key
+
+
+def local(queries, keys, values, query_weight, key_weight):
+    rows, local_heads, width = queries.shape
+    shards = lax.axis_size("seq")
+    fits = shards <= LIMIT and shards % 2 == 0 and local_heads == 2 and rows == width == 128
+    if fits and 2 * query_weight.shape[1] == width:
+        return local_gathered(queries, keys, values, query_weight, key_weight)
+    return local_general(queries, keys, values, query_weight, key_weight)
+
+
 def solution(mesh):
     in_specs = (
         P(("rep", "seq"), "head", None),

time: 130 us -> 35.7 us (0.27)
  blocking collectives: 91.5 us -> 0 us
  between operations: 14.8 us -> 0.69 us
  waiting for transfers between devices: 0.02 us -> 10.1 us
  Pallas kernels: 0 us -> 8.02 us
  matrix products: 7.72 us -> 0 us
  starting transfers between devices: 8.47 us -> 13.4 us
  local copies, waits for them, and re-layouts: 4.81 us -> 3.29 us
  other arithmetic: 1.51 us -> 0.01 us
    all_gather x4 -> x0, blocking collectives: 51.8 us -> none  [the longest x2 24.9 us: prefix_2(): everything = jax.tree.map(lambda part: lax.all_gather(part, axis), x)]
    psum x1 -> x0, blocking collectives: 39.7 us -> none  [local(): loss = lax.psum(loss_part, ('seq', 'head')).reshape(1)]
    ppermute x2 -> x8, waiting for transfers between devices: 0.01 us -> 10.1 us  [the longest x6 8.34 us: local_gathered(): lax.ppermute(x, axis, [(i, (i + d) % size) for i in range(size)])]
    pallas_call x0 -> x3, Pallas kernels: none -> 8.02 us  [the longest x1 4.65 us: local_gathered(): pl.pallas_call(functools.partial(main_kernel, shards, rows), out_shape=(s...]
    dot_general x18 -> x0, matrix products: 7.47 us -> none  [the longest x1 0.85 us: local(): jnp.einsum('hjf,jd->hfd', key_act_grad, ext_keys_wide, precision=exact)]
    ppermute x2 -> x8, starting transfers between devices: 8.43 us -> 13.4 us  [the longest x6 9.64 us: local_gathered(): lax.ppermute(x, axis, [(i, (i + d) % size) for i in range(size)])]
  transfers between devices with their start and end apart: 3 -> 8, of which waited for: 0 -> 5; matrix products, arithmetic and copies ran while one was open for 3% -> 0% of each run, Pallas kernels for 0% -> 0%
where the time goes in v1:
time: 35.7 us; the launch traced here: 35.5 us
  starting transfers between devices  13.4 us (38%)
  waiting for transfers between devices  10.1 us (28%)
  Pallas kernels  8.02 us (22%)
  local copies, waits for them, and re-layouts  3.29 us (9%)
  between operations  0.69 us (2%)
    ppermute x6, starting transfers between devices, local_gathered(): lax.ppermute(x, axis, [(i, (i + d) % size) for i in range(size)])  9.64 us
    ppermute x6, waiting for transfers between devices, local_gathered(): lax.ppermute(x, axis, [(i, (i + d) % size) for i in range(size)])  8.34 us
    pallas_call x1, Pallas kernels, local_gathered(): pl.pallas_call(functools.partial(main_kernel, shards, rows), out_shape=(s...  4.65 us
    ppermute x2, starting transfers between devices, local_gathered(): swap = lambda x: lax.ppermute(x, 'seq', [(i, i ^ 1) for i in range(shards)])  3.74 us
    unnamed x14, local copies, waits for them, and re-layouts  2.11 us
    pallas_call x1, Pallas kernels, local_gathered(): pl.pallas_call(pack_kernel, out_shape=(shape((3 * rows, width), bf16),) *...  1.83 us
    ppermute x2, waiting for transfers between devices, local_gathered(): swap = lambda x: lax.ppermute(x, 'seq', [(i, i ^ 1) for i in range(shards)])  1.74 us
    pallas_call x1, Pallas kernels, local_gathered(): pl.pallas_call(join_kernel, out_shape=(shape((local_heads, features, widt...  1.54 us
  transfers between devices with their start and end apart: 8, of which 5 were waited for; matrix products, arithmetic and copies ran while one was open for 0% of the time, Pallas kernels for 0%

profile of v1, /device:TPU:0, one launch (start us, length us, event | category | flops | bytes accessed | tf_op | source)
XLA Modules:
  0.0 35.5 jit_solution(2087573865735016216)
XLA Ops:
  0.6 0.0 copy-start.3
  0.6 0.0 copy-start.2
  0.7 1.8 %pack.1 = (bf16[384,128]{1,0:T(8,128)(2,1)}, bf16[384,128]{1,0:T(8,128)(2,1)}) custom-call(bf16[128,2,128]{2,1,0:T(2,128)(2,1)} %queries_ref.1, bf16[128,128]{1,0:T(8,128)(2,1)} %keys_ref.1, bf16[128,128]{1,0:T(8,128)(2,1)} %values_ref.1), custom_call_target="tpu_custom_call" | custom-call | tf_op jit(solution)/shard_map/pack/pallas_call | solution.py:429
  2.5 4.1 %collective-permute-start.1 = (bf16[384,128]{1,0:T(8,128)(2,1)}, bf16[384,128]{1,0:T(8,128)(2,1)S(1)}, u32[]{:S(2)}, u32[]{:S(2)}) collective-permute-start(bf16[384,128]{1,0:T(8,128)(2,1)} %get-tuple-element.10.refs_0_), channel_id=1, source_target_pairs={{0,16},{8,24},{16,0},{24,8},{1,17},{9,25},{17,1},{25,9},{2,18},{10... | collective-permute-start | bytes 294920 | tf_op jit(solution)/shard_map/ppermute | solution.py:436
  6.5 1.3 %collective-permute-start.2 = (bf16[384,128]{1,0:T(8,128)(2,1)}, bf16[384,128]{1,0:T(8,128)(2,1)S(1)}, u32[]{:S(2)}, u32[]{:S(2)}) collective-permute-start(bf16[384,128]{1,0:T(8,128)(2,1)} %get-tuple-element.11), channel_id=1, source_target_pairs={{0,24},{8,0},{16,8},{24,16},{1,25},{9,1},{17,9},{25,17},{2,26},{10... | collective-permute-start | bytes 294920 | tf_op jit(solution)/shard_map/ppermute | solution.py:436
  7.9 0.7 %collective-permute-start = (bf16[384,128]{1,0:T(8,128)(2,1)}, bf16[384,128]{1,0:T(8,128)(2,1)S(1)}, u32[]{:S(2)}, u32[]{:S(2)}) collective-permute-start(bf16[384,128]{1,0:T(8,128)(2,1)} %get-tuple-element.11), channel_id=1, source_target_pairs={{0,8},{8,16},{16,24},{24,0},{1,9},{9,17},{17,25},{25,1},{2,10},{10... | collective-permute-start | bytes 294920 | tf_op jit(solution)/shard_map/ppermute | solution.py:436
  8.6 4.6 %collective-permute-done.1.refs_2_ = bf16[384,128]{1,0:T(8,128)(2,1)S(1)} collective-permute-done((bf16[384,128]{1,0:T(8,128)(2,1)}, bf16[384,128]{1,0:T(8,128)(2,1)S(1)}, u32[]{:S(2)}, u32[]{:S(2)}) %collective-permute-start.1) | collective-permute-done | bytes 98336 | tf_op jit(solution)/shard_map/ppermute | solution.py:436
  13.2 0.0 collective-permute-done.2.refs_3_
  13.2 1.7 %collective-permute-done.refs_1_ = bf16[384,128]{1,0:T(8,128)(2,1)S(1)} collective-permute-done((bf16[384,128]{1,0:T(8,128)(2,1)}, bf16[384,128]{1,0:T(8,128)(2,1)S(1)}, u32[]{:S(2)}, u32[]{:S(2)}) %collective-permute-start) | collective-permute-done | bytes 98336 | tf_op jit(solution)/shard_map/ppermute | solution.py:436
  14.9 0.0 copy-done.3
  14.9 0.0 copy-done.2
  14.9 0.0 copy-start
  14.9 0.9 %copy-done = bf16[384,128]{1,0:T(8,128)(2,1)S(1)} copy-done((bf16[384,128]{1,0:T(8,128)(2,1)S(1)}, bf16[384,128]{1,0:T(8,128)(2,1)}, u32[]{:S(2)}) %copy-start) | copy-done | bytes 98328
  15.8 4.6 %main.1 = (f32[128,128]{1,0:T(8,128)S(1)}, f32[8,128]{1,0:T(8,128)S(1)}) custom-call(bf16[384,128]{1,0:T(8,128)(2,1)S(1)} %copy-done, bf16[384,128]{1,0:T(8,128)(2,1)S(1)} %collective-permute-done.refs_1_, bf16[384,128]{1,0:T(8,128)(2,1)S(1)} %collective-permute-done.1.refs_2_, bf16[384,128]{1,0:T(8,128)(2,1)S(1)} %collective-permute-done.2.refs_3_, ...), custom_call_target="tpu_custom_call" | custom-call | tf_op jit(solution)/shard_map/main/pallas_call | solution.py:438
  20.4 0.0 copy-start.1
  20.4 2.5 %collective-permute-start.6 = (f32[8,128]{1,0:T(8,128)S(1)}, f32[8,128]{1,0:T(8,128)S(1)}, u32[]{:S(2)}, u32[]{:S(2)}) collective-permute-start(f32[8,128]{1,0:T(8,128)S(1)} %get-tuple-element.13), channel_id=1, source_target_pairs={{0,6},{2,0},{4,2},{6,4},{1,7},{3,1},{5,3},{7,5},{8,14},{10,8},{12,... | collective-permute-start | bytes 12296 | tf_op jit(solution)/shard_map/ppermute | solution.py:436
  22.9 0.5 %collective-permute-start.5 = (f32[8,128]{1,0:T(8,128)S(1)}, f32[8,128]{1,0:T(8,128)S(1)}, u32[]{:S(2)}, u32[]{:S(2)}) collective-permute-start(f32[8,128]{1,0:T(8,128)S(1)} %get-tuple-element.13), channel_id=1, source_target_pairs={{0,4},{2,6},{4,0},{6,2},{1,5},{3,7},{5,1},{7,3},{8,12},{10,14},{12... | collective-permute-start | bytes 12296 | tf_op jit(solution)/shard_map/ppermute | solution.py:436
  23.4 0.6 %collective-permute-start.4 = (f32[8,128]{1,0:T(8,128)S(1)}, f32[8,128]{1,0:T(8,128)S(1)}, u32[]{:S(2)}, u32[]{:S(2)}) collective-permute-start(f32[8,128]{1,0:T(8,128)S(1)} %get-tuple-element.13), channel_id=1, source_target_pairs={{0,2},{2,4},{4,6},{6,0},{1,3},{3,5},{5,7},{7,1},{8,10},{10,12},{12... | collective-permute-start | bytes 12296 | tf_op jit(solution)/shard_map/ppermute | solution.py:436
  24.0 1.9 %collective-permute-start.3 = (f32[128,128]{1,0:T(8,128)S(1)}, f32[128,128]{1,0:T(8,128)S(1)}, u32[]{:S(2)}, u32[]{:S(2)}) collective-permute-start(f32[128,128]{1,0:T(8,128)S(1)} %get-tuple-element.12.own_ref), channel_id=1, source_target_pairs={{0,8},{8,0},{16,24},{24,16},{1,9},{9,1},{17,25},{25,17},{2,10},{10... | collective-permute-start | bytes 196616 | tf_op jit(solution)/shard_map/ppermute | solution.py:454
  25.9 0.0 collective-permute-done.6
  25.9 0.6 %collective-permute-done.5 = f32[8,128]{1,0:T(8,128)S(1)} collective-permute-done((f32[8,128]{1,0:T(8,128)S(1)}, f32[8,128]{1,0:T(8,128)S(1)}, u32[]{:S(2)}, u32[]{:S(2)}) %collective-permute-start.5) | collective-permute-done | bytes 4128 | tf_op jit(solution)/shard_map/ppermute | solution.py:436
  26.5 1.4 %collective-permute-done.4 = f32[8,128]{1,0:T(8,128)S(1)} collective-permute-done((f32[8,128]{1,0:T(8,128)S(1)}, f32[8,128]{1,0:T(8,128)S(1)}, u32[]{:S(2)}, u32[]{:S(2)}) %collective-permute-start.4) | collective-permute-done | bytes 4128 | tf_op jit(solution)/shard_map/ppermute | solution.py:436
  27.9 0.0 copy-start.5
  27.9 1.9 %collective-permute-start.7 = (f32[8,128]{1,0:T(8,128)S(1)}, f32[8,128]{1,0:T(8,128)S(1)}, u32[]{:S(2)}, u32[]{:S(2)}) collective-permute-start(f32[8,128]{1,0:T(8,128)S(1)} %add_add_fusion.loss_a_ref), channel_id=1, source_target_pairs={{0,8},{8,0},{16,24},{24,16},{1,9},{9,1},{17,25},{25,17},{2,10},{10... | collective-permute-start | bytes 12296 | tf_op jit(solution)/shard_map/ppermute | solution.py:454
  29.8 1.7 %collective-permute-done.7.loss_b_ref = f32[8,128]{1,0:T(8,128)S(1)} collective-permute-done((f32[8,128]{1,0:T(8,128)S(1)}, f32[8,128]{1,0:T(8,128)S(1)}, u32[]{:S(2)}, u32[]{:S(2)}) %collective-permute-start.7) | collective-permute-done | bytes 4128 | tf_op jit(solution)/shard_map/ppermute | solution.py:454
  31.5 0.0 copy-start.6
  31.5 0.0 collective-permute-done.3.other_ref
  31.5 0.0 copy-done.1
  31.5 0.0 copy-done.5
  31.5 0.6 %copy-done.6 = f32[8,128]{1,0:T(8,128)} copy-done((f32[8,128]{1,0:T(8,128)}, f32[8,128]{1,0:T(8,128)S(1)}, u32[]{:S(2)}) %copy-start.6) | copy-done | bytes 4120
  32.1 0.0 copy-start.4
  32.1 0.6 %copy-done.4 = f32[128,128]{1,0:T(8,128)} copy-done((f32[128,128]{1,0:T(8,128)}, f32[128,128]{1,0:T(8,128)S(1)}, u32[]{:S(2)}) %copy-start.4) | copy-done | bytes 65560
  32.7 1.5 %join.1 = (f32[2,64,128]{2,1,0:T(8,128)}, f32[2,64,128]{2,1,0:T(8,128)}, f32[8,128]{1,0:T(8,128)}) custom-call(f32[128,128]{1,0:T(8,128)} %copy-done.1, f32[128,128]{1,0:T(8,128)} %copy-done.4, f32[8,128]{1,0:T(8,128)} %copy-done.5, f32[8,128]{1,0:T(8,128)} %copy-done.6), custom_call_target="tpu_custom_call" | custom-call | tf_op jit(solution)/shard_map/join/pallas_call | solution.py:458
  34.3 1.2 %slice.3 = f32[1,1]{1,0:T(1,128)} slice(f32[8,128]{1,0:T(8,128)} %get-tuple-element.14), slice={[0:1], [0:1]} | slice | bytes 8 | tf_op jit(solution)/shard_map/slice | solution.py:465
  (1 shorter events, 0.0 us)
Async XLA Ops:
  0.6 14.2 %copy-start.3 = (f32[2,64,128]{2,1,0:T(8,128)S(1)}, f32[2,64,128]{2,1,0:T(8,128)}, u32[]{:S(2)}) copy-start(f32[2,64,128]{2,1,0:T(8,128)} %refs_5_.1) | copy-start | bytes 196612
  0.6 14.2 %copy-start.2 = (f32[2,64,128]{2,1,0:T(8,128)S(1)}, f32[2,64,128]{2,1,0:T(8,128)}, u32[]{:S(2)}) copy-start(f32[2,64,128]{2,1,0:T(8,128)} %refs_4_.1) | copy-start | bytes 196612
  2.5 10.7 %collective-permute-start.1 = (bf16[384,128]{1,0:T(8,128)(2,1)}, bf16[384,128]{1,0:T(8,128)(2,1)S(1)}, u32[]{:S(2)}, u32[]{:S(2)}) collective-permute-start(bf16[384,128]{1,0:T(8,128)(2,1)} %get-tuple-element.10.refs_0_), channel_id=1, source_target_pairs={{0,16},{8,24},{16,0},{24,8},{1,17},{9,25},{17,1},{25,9},{2,18},{10... | collective-permute-start | bytes 294920 | tf_op jit(solution)/shard_map/ppermute | solution.py:436
  6.5 6.6 %collective-permute-start.2 = (bf16[384,128]{1,0:T(8,128)(2,1)}, bf16[384,128]{1,0:T(8,128)(2,1)S(1)}, u32[]{:S(2)}, u32[]{:S(2)}) collective-permute-start(bf16[384,128]{1,0:T(8,128)(2,1)} %get-tuple-element.11), channel_id=1, source_target_pairs={{0,24},{8,0},{16,8},{24,16},{1,25},{9,1},{17,9},{25,17},{2,26},{10... | collective-permute-start | bytes 294920 | tf_op jit(solution)/shard_map/ppermute | solution.py:436
  7.9 7.0 %collective-permute-start = (bf16[384,128]{1,0:T(8,128)(2,1)}, bf16[384,128]{1,0:T(8,128)(2,1)S(1)}, u32[]{:S(2)}, u32[]{:S(2)}) collective-permute-start(bf16[384,128]{1,0:T(8,128)(2,1)} %get-tuple-element.11), channel_id=1, source_target_pairs={{0,8},{8,16},{16,24},{24,0},{1,9},{9,17},{17,25},{25,1},{2,10},{10... | collective-permute-start | bytes 294920 | tf_op jit(solution)/shard_map/ppermute | solution.py:436
  14.9 0.9 %copy-start = (bf16[384,128]{1,0:T(8,128)(2,1)S(1)}, bf16[384,128]{1,0:T(8,128)(2,1)}, u32[]{:S(2)}) copy-start(bf16[384,128]{1,0:T(8,128)(2,1)} %get-tuple-element.10.refs_0_) | copy-start | bytes 294916
  20.4 11.1 %copy-start.1 = (f32[128,128]{1,0:T(8,128)}, f32[128,128]{1,0:T(8,128)S(1)}, u32[]{:S(2)}) copy-start(f32[128,128]{1,0:T(8,128)S(1)} %get-tuple-element.12.own_ref) | copy-start | bytes 196612
  20.4 5.4 %collective-permute-start.6 = (f32[8,128]{1,0:T(8,128)S(1)}, f32[8,128]{1,0:T(8,128)S(1)}, u32[]{:S(2)}, u32[]{:S(2)}) collective-permute-start(f32[8,128]{1,0:T(8,128)S(1)} %get-tuple-element.13), channel_id=1, source_target_pairs={{0,6},{2,0},{4,2},{6,4},{1,7},{3,1},{5,3},{7,5},{8,14},{10,8},{12,... | collective-permute-start | bytes 12296 | tf_op jit(solution)/shard_map/ppermute | solution.py:436
  22.9 3.6 %collective-permute-start.5 = (f32[8,128]{1,0:T(8,128)S(1)}, f32[8,128]{1,0:T(8,128)S(1)}, u32[]{:S(2)}, u32[]{:S(2)}) collective-permute-start(f32[8,128]{1,0:T(8,128)S(1)} %get-tuple-element.13), channel_id=1, source_target_pairs={{0,4},{2,6},{4,0},{6,2},{1,5},{3,7},{5,1},{7,3},{8,12},{10,14},{12... | collective-permute-start | bytes 12296 | tf_op jit(solution)/shard_map/ppermute | solution.py:436
  23.4 4.5 %collective-permute-start.4 = (f32[8,128]{1,0:T(8,128)S(1)}, f32[8,128]{1,0:T(8,128)S(1)}, u32[]{:S(2)}, u32[]{:S(2)}) collective-permute-start(f32[8,128]{1,0:T(8,128)S(1)} %get-tuple-element.13), channel_id=1, source_target_pairs={{0,2},{2,4},{4,6},{6,0},{1,3},{3,5},{5,7},{7,1},{8,10},{10,12},{12... | collective-permute-start | bytes 12296 | tf_op jit(solution)/shard_map/ppermute | solution.py:436
  24.0 7.5 %collective-permute-start.3 = (f32[128,128]{1,0:T(8,128)S(1)}, f32[128,128]{1,0:T(8,128)S(1)}, u32[]{:S(2)}, u32[]{:S(2)}) collective-permute-start(f32[128,128]{1,0:T(8,128)S(1)} %get-tuple-element.12.own_ref), channel_id=1, source_target_pairs={{0,8},{8,0},{16,24},{24,16},{1,9},{9,1},{17,25},{25,17},{2,10},{10... | collective-permute-start | bytes 196616 | tf_op jit(solution)/shard_map/ppermute | solution.py:454
  27.9 3.6 %copy-start.5 = (f32[8,128]{1,0:T(8,128)}, f32[8,128]{1,0:T(8,128)S(1)}, u32[]{:S(2)}) copy-start(f32[8,128]{1,0:T(8,128)S(1)} %add_add_fusion.loss_a_ref) | copy-start | bytes 12292
  27.9 3.6 %collective-permute-start.7 = (f32[8,128]{1,0:T(8,128)S(1)}, f32[8,128]{1,0:T(8,128)S(1)}, u32[]{:S(2)}, u32[]{:S(2)}) collective-permute-start(f32[8,128]{1,0:T(8,128)S(1)} %add_add_fusion.loss_a_ref), channel_id=1, source_target_pairs={{0,8},{8,0},{16,24},{24,16},{1,9},{9,1},{17,25},{25,17},{2,10},{10... | collective-permute-start | bytes 12296 | tf_op jit(solution)/shard_map/ppermute | solution.py:454
  31.5 0.6 %copy-start.6 = (f32[8,128]{1,0:T(8,128)}, f32[8,128]{1,0:T(8,128)S(1)}, u32[]{:S(2)}) copy-start(f32[8,128]{1,0:T(8,128)S(1)} %collective-permute-done.7.loss_b_ref) | copy-start | bytes 12292
  32.1 0.6 %copy-start.4 = (f32[128,128]{1,0:T(8,128)}, f32[128,128]{1,0:T(8,128)S(1)}, u32[]{:S(2)}) copy-start(f32[128,128]{1,0:T(8,128)S(1)} %collective-permute-done.3.other_ref) | copy-start | bytes 196612

commit v2 on v1

--- a/solution.py
+++ b/solution.py
@@ -15,6 +15,7 @@
 f32, bf16 = jnp.float32, jnp.bfloat16
 PAD = 16
 LIMIT = 8
+SMALL, LARGE = 4 << 20, 24 << 20
 
 
 def shifted(value, axis, steps):
@@ -241,7 +242,7 @@
     return lax.broadcasted_iota(jnp.int32, shape, axis)
 
 
-def head_pass(queries, keys, values, ext_keys, ext_values, ext_keys_t, values_t, ext_aug_t, ext_aug, pair_sum, query_weight, key_weight, block, tokens_total):
+def forward_pass(queries, keys, ext_keys, values_t, ext_aug_t, pair_sum, query_weight, key_weight, block, tokens_total):
     tokens, width = queries.shape
     blocks = tokens // block
     scale = width ** (-0.5)
@@ -252,16 +253,12 @@
     raised = jnp.exp(dot_t(ext_keys, wk[0]) + dot_t(ext_keys, wk[1]))
     kf = raised / dot_left(split(raised), pair_sum)
     kf = jnp.where(iota(kf.shape, 0) >= WINDOW, kf, 0.0)
-    qf = qf_t.T
-    kf_t = kf.T
-    qf_ts, kf_s, qf_s, kf_ts = split(qf_t), split(kf), split(qf), split(kf_t)
+    qf_ts, kf_s = split(qf_t), split(kf)
     tri = iota((block, block), 0) <= iota((block, block), 1)
     near = iota((block + WINDOW, block), 0) > iota((block + WINDOW, block), 1)
     loss = jnp.zeros((1, 1), f32)
     state_t = None
-    state = None
-    saved = []
-    cut = lambda pair, at: tuple(part[at] for part in pair)
+    nums, dens = [], []
     for b in range(blocks):
         lo, hi = b * block, (b + 1) * block
         here = (slice(None), slice(lo, hi))
@@ -297,21 +294,35 @@
         aug = dot_right(ext_aug_t[:, lo:hi], split(linear))
         if b:
             aug = aug + dot3(split(state_t), cut(qf_ts, here))
-        saved_state = state
         if b + 1 < blocks:
             grown_t = dot_right(ext_aug_t[:, lo:hi], cut(kf_s, rows))
-            grown = dot_left(cut(kf_ts, here), ext_aug[lo:hi])
             state_t = grown_t if state_t is None else state_t + grown_t
-            state = grown if state is None else state + grown
         lift = jnp.exp(-wbest)
         over = 1.0 / (wtotal + lift * aug[width : width + 1])
         student = (wsum + lift * aug[:width]) * over
         difference = student - teacher
         loss = loss + jnp.sum(jnp.sum(difference * difference, axis=0, keepdims=True), axis=1, keepdims=True)
         grad = difference * (2.0 / tokens_total)
-        num = grad * (lift * over)
-        den = -(lift * over) * jnp.sum(grad * student, axis=0, keepdims=True)
-        saved.append((num, den, saved_state))
+        nums.append(grad * (lift * over))
+        dens.append(-(lift * over) * jnp.sum(grad * student, axis=0, keepdims=True))
+    return loss, qf_t, kf, nums, dens
+
+
+def cut(pair, at):
+    return tuple(part[at] for part in pair)
+
+
+def backward_pass(qf_t, kf, nums, dens, queries, ext_values, ext_keys_t, pair_sum, block):
+    width, tokens = queries.shape[1], queries.shape[0]
+    blocks = tokens // block
+    tri = iota((block, block), 0) <= iota((block, block), 1)
+    qf_s, kf_ts = split(qf_t.T), split(kf.T)
+    ext_aug = jnp.concatenate([ext_values, (iota((tokens, width), 1) == 0).astype(bf16)], axis=1)
+    states = [None]
+    for b in range(blocks - 1):
+        lo, hi = b * block, (b + 1) * block
+        grown = dot_left(cut(kf_ts, (slice(None), slice(lo, hi))), ext_aug[lo:hi])
+        states.append(grown if b == 0 else states[-1] + grown)
     grad_q = jnp.zeros((qf_t.shape[0], width), f32)
     grad_k = jnp.zeros((width, kf.shape[1]), f32)
     later = None
@@ -319,13 +330,13 @@
         lo, hi = b * block, (b + 1) * block
         here = (slice(None), slice(lo, hi))
         rows = (slice(lo, hi), slice(None))
-        num, den, state_b = saved[b]
+        num, den = nums[b], dens[b]
         num_s = split(num)
         link = jnp.where(tri, dot_right(ext_values[lo:hi], num_s) + den, 0.0)
         link_s = split(link)
         qfg = dot3(cut(kf_ts, here), link_s)
         if b:
-            qfg = qfg + dot3(split(state_b[:, :width]), num_s) + state_b[:, width : width + 1] * den
+            qfg = qfg + dot3(split(states[b][:, :width]), num_s) + states[b][:, width : width + 1] * den
         kfg = dot3(link_s, cut(qf_s, rows))
         if later is not None:
             kfg = kfg + dot_right(ext_values[lo:hi], split(later[:width])) + later[width : width + 1]
@@ -341,36 +352,47 @@
         grad_k = grad_k + dot_right(ext_keys_t[:, lo:hi], split(back))
     half = grad_q.shape[0] // 2
     grad_k = grad_k.T
-    return loss, grad_q[:half] - grad_q[half:], grad_k[:half] - grad_k[half:]
-
-
-def shared_parts(keys, values, ext_keys, ext_values, features):
-    tokens, width = keys.shape
-    eye = (iota((width, width), 0) == iota((width, width), 1)).astype(bf16)
-    turn = lambda x: dot_t(eye, x).astype(bf16)
-    values_t = turn(values)
-    ext_keys_t = turn(ext_keys)
-    ones = (iota((PAD, tokens), 0) == 0).astype(bf16)
-    ext_aug_t = jnp.concatenate([turn(ext_values), ones], axis=0)
-    ext_aug = jnp.concatenate([ext_values, (iota((tokens, width), 1) == 0).astype(bf16)], axis=1)
+    return grad_q[:half] - grad_q[half:], grad_k[:half] - grad_k[half:]
+
+
+def turned(x):
+    eye = (iota((x.shape[1], x.shape[1]), 0) == iota((x.shape[1], x.shape[1]), 1)).astype(bf16)
+    return dot_t(eye, x).astype(bf16)
+
+
+def with_ones(x_t):
+    return jnp.concatenate([x_t, (iota((PAD, x_t.shape[1]), 0) == 0).astype(bf16)], axis=0)
+
+
+def pair_sums(features):
     half = features // 2
-    pair_sum = ((iota((features, features), 0) < half) == (iota((features, features), 1) < half)).astype(bf16)
-    return values_t, ext_keys_t, ext_aug_t, ext_aug, pair_sum
-
-
-def pack_kernel(queries_ref, keys_ref, values_ref, same_ref, other_ref):
+    return ((iota((features, features), 0) < half) == (iota((features, features), 1) < half)).astype(bf16)
+
+
+def pack_kernel(queries_ref, keys_ref, values_ref, same_ref, other_ref, queries_in, sems):
     rows = keys_ref.shape[0]
+    copies = [
+        pltpu.make_async_copy(queries_ref, queries_in, sems.at[0]),
+        pltpu.make_async_copy(keys_ref, same_ref.at[pl.ds(0, rows)], sems.at[1]),
+        pltpu.make_async_copy(values_ref, same_ref.at[pl.ds(rows, rows)], sems.at[2]),
+        pltpu.make_async_copy(keys_ref, other_ref.at[pl.ds(0, rows)], sems.at[3]),
+        pltpu.make_async_copy(values_ref, other_ref.at[pl.ds(rows, rows)], sems.at[4]),
+    ]
+    for copy in copies:
+        copy.start()
     odd = lax.rem(lax.axis_index("seq"), 2) == 1
-    first, second = queries_ref[:, 0, :], queries_ref[:, 1, :]
-    for ref, chosen in ((same_ref, jnp.where(odd, second, first)), (other_ref, jnp.where(odd, first, second))):
-        ref[:rows] = keys_ref[...]
-        ref[rows : 2 * rows] = values_ref[...]
-        ref[2 * rows :] = chosen
-
-
-def main_kernel(shards, rows, *refs):
+    copies[0].wait()
+    first, second = queries_in[:, 0, :], queries_in[:, 1, :]
+    same_ref[2 * rows :] = jnp.where(odd, second, first)
+    other_ref[2 * rows :] = jnp.where(odd, first, second)
+    for copy in copies[1:]:
+        copy.wait()
+
+
+def forward_kernel(shards, rows, *refs):
     blocks_in = refs[:shards]
-    query_weight_ref, key_weight_ref, grads_ref, loss_ref, keys_ref, values_ref, queries_ref, qw_ref, kw_ref, sems = refs[shards:]
+    query_weight_ref, key_weight_ref, loss_ref, keys_ref, values_ref, queries_ref, qf_ref, kf_ref, num_ref, den_ref = refs[shards : shards + 10]
+    qw_ref, kw_ref, sems = refs[shards + 10 :]
     tokens, width = queries_ref.shape
     place = lax.axis_index("seq")
     mine = lax.rem(place, 2)
@@ -392,30 +414,45 @@
     values_ref[:WINDOW] = jnp.zeros((WINDOW, width), bf16)
     for copy in copies:
         copy.wait()
-    keys, values = keys_ref[WINDOW:], values_ref[WINDOW:]
-    ext_keys, ext_values = keys_ref[:tokens], values_ref[:tokens]
-    values_t, ext_keys_t, ext_aug_t, ext_aug, pair_sum = shared_parts(
-        keys, values, ext_keys, ext_values, 2 * qw_ref.shape[0]
-    )
-    block = 256 if tokens % 256 == 0 else 128
-    loss, grad_q, grad_k = head_pass(
-        queries_ref[...], keys, values, ext_keys, ext_values, ext_keys_t, values_t, ext_aug_t, ext_aug, pair_sum,
-        qw_ref[...], kw_ref[...], block, tokens,
-    )
-    half = qw_ref.shape[0]
-    grads_ref[:half] = grad_q
-    grads_ref[half:] = grad_k
+    block = block_of(tokens)
+    loss, qf_t, kf, nums, dens = forward_pass(
+        queries_ref[...], keys_ref[WINDOW:], keys_ref[:tokens], turned(values_ref[WINDOW:]),
+        with_ones(turned(values_ref[:tokens])), pair_sums(2 * qw_ref.shape[0]), qw_ref[...], kw_ref[...], block, tokens,
+    )
+    qf_ref[...] = qf_t
+    kf_ref[...] = kf
+    for b in range(tokens // block):
+        at = slice(b * block, (b + 1) * block)
+        num_ref[:, at] = nums[b]
+        den_ref[:, at] = jnp.broadcast_to(dens[b], (8, block))
     loss_ref[...] = jnp.broadcast_to(loss / tokens, loss_ref.shape)
 
 
-def join_kernel(own_ref, other_ref, loss_a_ref, loss_b_ref, grad_q_ref, grad_k_ref, loss_ref):
+def block_of(tokens):
+    return 256 if tokens % 256 == 0 else 128
+
+
+def backward_kernel(keys_ref, values_ref, queries_ref, qf_ref, kf_ref, num_ref, den_ref, grads_ref):
+    tokens = queries_ref.shape[0]
+    half = qf_ref.shape[0] // 2
+    block = block_of(tokens)
+    cuts = [slice(b * block, (b + 1) * block) for b in range(tokens // block)]
+    grads_ref[:half], grads_ref[half:] = backward_pass(
+        qf_ref[...], kf_ref[...], [num_ref[:, at] for at in cuts], [den_ref[:1, at] for at in cuts],
+        queries_ref[...], values_ref[:tokens], turned(keys_ref[:tokens]), pair_sums(2 * half), block,
+    )
+
+
+def join_kernel(own_ref, other_ref, *refs):
+    loss_refs = refs[:-3]
+    grad_q_ref, grad_k_ref, loss_ref = refs[-3:]
     half = grad_q_ref.shape[1]
     odd = lax.rem(lax.axis_index("seq"), 2) == 1
     own, other = own_ref[...], other_ref[...]
     first, second = jnp.where(odd, other, own), jnp.where(odd, own, other)
     grad_q_ref[0], grad_q_ref[1] = first[:half], second[:half]
     grad_k_ref[0], grad_k_ref[1] = first[half:], second[half:]
-    loss_ref[...] = loss_a_ref[...] + loss_b_ref[...]
+    loss_ref[0] = sum(ref[0, 0] for ref in loss_refs)
 
 
 def local_gathered(queries, keys, values, query_weight, key_weight):
@@ -429,40 +466,59 @@
     same, other = pl.pallas_call(
         pack_kernel,
         out_shape=(shape((3 * rows, width), bf16),) * 2,
-        in_specs=[vmem] * 3,
+        in_specs=[pl.BlockSpec(memory_space=pltpu.HBM)] * 3,
         out_specs=(vmem,) * 2,
+        scratch_shapes=[pltpu.VMEM(queries.shape, bf16), pltpu.SemaphoreType.DMA((5,))],
+        compiler_params=pltpu.CompilerParams(vmem_limit_bytes=SMALL),
         name="pack",
-    )(queries, keys, values)
+    )(*(pltpu.with_memory_space_constraint(x, pltpu.HBM) for x in (queries, keys, values)))
     turn = lambda x, axis, size, d: lax.ppermute(x, axis, [(i, (i + d) % size) for i in range(size)])
     pieces = [same] + [turn(other if d % 2 else same, "seq", shards, d) for d in range(1, shards)]
-    grads, loss = pl.pallas_call(
-        functools.partial(main_kernel, shards, rows),
-        out_shape=(shape((2 * features, width), f32), shape((8, 128), f32)),
+    loss, *kept = pl.pallas_call(
+        functools.partial(forward_kernel, shards, rows),
+        out_shape=(
+            shape((8, 128), f32),
+            shape((tokens + WINDOW, width), bf16),
+            shape((tokens + WINDOW, width), bf16),
+            shape((tokens, width), bf16),
+            shape((2 * features, tokens), f32),
+            shape((tokens, 2 * features), f32),
+            shape((width, tokens), f32),
+            shape((8, tokens), f32),
+        ),
         in_specs=[anywhere] * (shards + 2),
-        out_specs=(vmem,) * 2,
+        out_specs=(vmem,) * 8,
         scratch_shapes=[
-            pltpu.VMEM((tokens + WINDOW, width), bf16),
-            pltpu.VMEM((tokens + WINDOW, width), bf16),
-            pltpu.VMEM((tokens, width), bf16),
             pltpu.VMEM((features, width), f32),
             pltpu.VMEM((features, width), f32),
             pltpu.SemaphoreType.DMA((3 * shards + 2,)),
         ],
-        compiler_params=pltpu.CompilerParams(vmem_limit_bytes=48 << 20),
-        name="main",
+        compiler_params=pltpu.CompilerParams(vmem_limit_bytes=LARGE),
+        cost_estimate=pl.CostEstimate(flops=10**9, bytes_accessed=10**7, transcendentals=10**6),
+        name="forward",
     )(*pieces, query_weight, key_weight)
     swap = lambda x: lax.ppermute(x, "seq", [(i, i ^ 1) for i in range(shards)])
     loss = sum((turn(loss, "head", columns, d) for d in range(1, columns)), loss)
+    grads = pl.pallas_call(
+        backward_kernel,
+        out_shape=shape((2 * features, width), f32),
+        in_specs=[vmem] * 7,
+        out_specs=vmem,
+        compiler_params=pltpu.CompilerParams(vmem_limit_bytes=LARGE),
+        cost_estimate=pl.CostEstimate(flops=10**9, bytes_accessed=10**7, transcendentals=10**6),
+        name="backward",
+    )(*kept)
     other_grads = swap(grads)
-    other_loss = swap(loss)
+    losses = [loss, swap(loss)]
     grad_query, grad_key, loss = pl.pallas_call(
         join_kernel,
-        out_shape=(shape((local_heads, features, width), f32),) * 2 + (shape((8, 128), f32),),
+        out_shape=(shape((local_heads, features, width), f32),) * 2 + (shape((1,), f32),),
         in_specs=[vmem] * 4,
-        out_specs=(vmem,) * 3,
+        out_specs=(vmem, vmem, pl.BlockSpec(memory_space=pltpu.SMEM)),
+        compiler_params=pltpu.CompilerParams(vmem_limit_bytes=SMALL),
         name="join",
-    )(grads, other_grads, loss, other_loss)
-    return loss[0, :1], grad_query, grad_key
+    )(grads, other_grads, *losses)
+    return loss, grad_query, grad_key
 
 
 def local(queries, keys, values, query_weight, key_weight):

time: 35.7 us -> 28.8 us (0.81)
  local copies, waits for them, and re-layouts: 3.29 us -> 0.01 us
  waiting for transfers between devices: 10.1 us -> 8.2 us
  Pallas kernels: 8.02 us -> 6.48 us
    unnamed x14 -> x4, local copies, waits for them, and re-layouts: 2.11 us -> 0.01 us
    ppermute x6, waiting for transfers between devices: 8.34 us -> 6.34 us  [local_gathered(): lax.ppermute(x, axis, [(i, (i + d) % size) for i in range(size)])]
    slice x1 -> x0, local copies, waits for them, and re-layouts: 1.18 us -> none  [local_gathered(): return (loss[0, :1], grad_query, grad_key)]
    pallas_call x1, Pallas kernels: 1.54 us -> 0.67 us  [local_gathered(): pl.pallas_call(join_kernel, out_shape=(shape((local_heads, features, widt...]
    pallas_call x1, Pallas kernels: 1.83 us -> 1.21 us  [local_gathered(): pl.pallas_call(pack_kernel, out_shape=(shape((3 * rows, width), bf16),) *...]
    pallas_call x1 -> x2, Pallas kernels: 4.65 us -> 4.59 us  [the longest x1 2.76 us: local_gathered(): pl.pallas_call(functools.partial(forward_kernel, shards, rows), out_shape...]
  transfers between devices with their start and end apart: 8 -> 8, of which waited for: 5 -> 4; matrix products, arithmetic and copies ran while one was open for 0% -> 0% of each run, Pallas kernels for 0% -> 6%
where the time goes in v2:
time: 28.8 us; the launch traced here: 28.7 us
  starting transfers between devices  13.3 us (46%)
  waiting for transfers between devices  8.2 us (28%)
  Pallas kernels  6.48 us (22%)
  between operations  0.68 us (2%)
    ppermute x6, starting transfers between devices, local_gathered(): lax.ppermute(x, axis, [(i, (i + d) % size) for i in range(size)])  9.71 us
    ppermute x6, waiting for transfers between devices, local_gathered(): lax.ppermute(x, axis, [(i, (i + d) % size) for i in range(size)])  6.34 us
    ppermute x2, starting transfers between devices, local_gathered(): swap = lambda x: lax.ppermute(x, 'seq', [(i, i ^ 1) for i in range(shards)])  3.58 us
    pallas_call x1, Pallas kernels, local_gathered(): pl.pallas_call(functools.partial(forward_kernel, shards, rows), out_shape...  2.76 us
    ppermute x2, waiting for transfers between devices, local_gathered(): swap = lambda x: lax.ppermute(x, 'seq', [(i, i ^ 1) for i in range(shards)])  1.85 us
    pallas_call x1, Pallas kernels, local_gathered(): pl.pallas_call(backward_kernel, out_shape=shape((2 * features, width), f3...  1.82 us
    pallas_call x1, Pallas kernels, local_gathered(): pl.pallas_call(pack_kernel, out_shape=(shape((3 * rows, width), bf16),) *...  1.21 us
    pallas_call x1, Pallas kernels, local_gathered(): pl.pallas_call(join_kernel, out_shape=(shape((local_heads, features, widt...  0.67 us
  transfers between devices with their start and end apart: 8, of which 4 were waited for; matrix products, arithmetic and copies ran while one was open for 0% of the time, Pallas kernels for 6%

profile of v2, /device:TPU:0, one launch (start us, length us, event | category | flops | bytes accessed | tf_op | source)
XLA Modules:
  0.0 28.7 jit_solution(3315641355823750511)
XLA Ops:
  0.6 0.0 copy-start.1
  0.6 0.0 copy-start
  0.7 1.2 %pack.1 = (bf16[384,128]{1,0:T(8,128)(2,1)S(1)}, bf16[384,128]{1,0:T(8,128)(2,1)S(1)}) custom-call(bf16[128,2,128]{2,1,0:T(2,128)(2,1)} %queries_ref.1, bf16[128,128]{1,0:T(8,128)(2,1)} %keys_ref.1, bf16[128,128]{1,0:T(8,128)(2,1)} %values_ref.1), custom_call_target="tpu_custom_call" | custom-call | tf_op jit(solution)/shard_map/pack/pallas_call | solution.py:466
  1.9 4.1 %collective-permute-start.1 = (bf16[384,128]{1,0:T(8,128)(2,1)S(1)}, bf16[384,128]{1,0:T(8,128)(2,1)S(1)}, u32[]{:S(2)}, u32[]{:S(2)}) collective-permute-start(bf16[384,128]{1,0:T(8,128)(2,1)S(1)} %get-tuple-element.16.refs_0_), channel_id=1, source_target_pairs={{0,16},{8,24},{16,0},{24,8},{1,17},{9,25},{17,1},{25,9},{2,18},{10... | collective-permute-start | bytes 294920 | tf_op jit(solution)/shard_map/ppermute | solution.py:475
  6.0 1.3 %collective-permute-start.2 = (bf16[384,128]{1,0:T(8,128)(2,1)S(1)}, bf16[384,128]{1,0:T(8,128)(2,1)S(1)}, u32[]{:S(2)}, u32[]{:S(2)}) collective-permute-start(bf16[384,128]{1,0:T(8,128)(2,1)S(1)} %get-tuple-element.17), channel_id=1, source_target_pairs={{0,24},{8,0},{16,8},{24,16},{1,25},{9,1},{17,9},{25,17},{2,26},{10... | collective-permute-start | bytes 294920 | tf_op jit(solution)/shard_map/ppermute | solution.py:475
  7.4 0.7 %collective-permute-start = (bf16[384,128]{1,0:T(8,128)(2,1)S(1)}, bf16[384,128]{1,0:T(8,128)(2,1)S(1)}, u32[]{:S(2)}, u32[]{:S(2)}) collective-permute-start(bf16[384,128]{1,0:T(8,128)(2,1)S(1)} %get-tuple-element.17), channel_id=1, source_target_pairs={{0,8},{8,16},{16,24},{24,0},{1,9},{9,17},{17,25},{25,1},{2,10},{10... | collective-permute-start | bytes 294920 | tf_op jit(solution)/shard_map/ppermute | solution.py:475
  8.0 4.4 %collective-permute-done.1.refs_2_ = bf16[384,128]{1,0:T(8,128)(2,1)S(1)} collective-permute-done((bf16[384,128]{1,0:T(8,128)(2,1)S(1)}, bf16[384,128]{1,0:T(8,128)(2,1)S(1)}, u32[]{:S(2)}, u32[]{:S(2)}) %collective-permute-start.1) | collective-permute-done | bytes 98336 | tf_op jit(solution)/shard_map/ppermute | solution.py:475
  12.4 0.0 collective-permute-done.2.refs_3_
  12.4 1.7 %collective-permute-done.refs_1_ = bf16[384,128]{1,0:T(8,128)(2,1)S(1)} collective-permute-done((bf16[384,128]{1,0:T(8,128)(2,1)S(1)}, bf16[384,128]{1,0:T(8,128)(2,1)S(1)}, u32[]{:S(2)}, u32[]{:S(2)}) %collective-permute-start) | collective-permute-done | bytes 98336 | tf_op jit(solution)/shard_map/ppermute | solution.py:475
  14.1 0.0 copy-done.1
  14.1 0.0 copy-done
  14.1 2.8 %forward.1 = (f32[8,128]{1,0:T(8,128)S(1)}, bf16[576,128]{1,0:T(8,128)(2,1)S(1)}, bf16[576,128]{1,0:T(8,128)(2,1)S(1)}, bf16[512,128]{1,0:T(8,128)(2,1)S(1)}, f3...) custom-call(bf16[384,128]{1,0:T(8,128)(2,1)S(1)} %get-tuple-element.16.refs_0_, ...), custom_call_target="tpu_custom_call" | custom-call | flops 1000000000 | bytes 10000000 | tf_op jit(solution)/shard_map/forward/pallas_call | solution.py:477
  16.9 2.5 %collective-permute-start.6 = (f32[8,128]{1,0:T(8,128)S(1)}, f32[8,128]{1,0:T(8,128)S(1)}, u32[]{:S(2)}, u32[]{:S(2)}) collective-permute-start(f32[8,128]{1,0:T(8,128)S(1)} %get-tuple-element.25), channel_id=1, source_target_pairs={{0,6},{2,0},{4,2},{6,4},{1,7},{3,1},{5,3},{7,5},{8,14},{10,8},{12,... | collective-permute-start | bytes 12296 | tf_op jit(solution)/shard_map/ppermute | solution.py:475
  19.4 0.5 %collective-permute-start.5 = (f32[8,128]{1,0:T(8,128)S(1)}, f32[8,128]{1,0:T(8,128)S(1)}, u32[]{:S(2)}, u32[]{:S(2)}) collective-permute-start(f32[8,128]{1,0:T(8,128)S(1)} %get-tuple-element.25), channel_id=1, source_target_pairs={{0,4},{2,6},{4,0},{6,2},{1,5},{3,7},{5,1},{7,3},{8,12},{10,14},{12... | collective-permute-start | bytes 12296 | tf_op jit(solution)/shard_map/ppermute | solution.py:475
  19.9 0.6 %collective-permute-start.4 = (f32[8,128]{1,0:T(8,128)S(1)}, f32[8,128]{1,0:T(8,128)S(1)}, u32[]{:S(2)}, u32[]{:S(2)}) collective-permute-start(f32[8,128]{1,0:T(8,128)S(1)} %get-tuple-element.25), channel_id=1, source_target_pairs={{0,2},{2,4},{4,6},{6,0},{1,3},{3,5},{5,7},{7,1},{8,10},{10,12},{12... | collective-permute-start | bytes 12296 | tf_op jit(solution)/shard_map/ppermute | solution.py:475
  20.5 1.8 %backward.1.own_ref = f32[128,128]{1,0:T(8,128)S(1)} custom-call(bf16[576,128]{1,0:T(8,128)(2,1)S(1)} %get-tuple-element.18.keys_ref, bf16[576,128]{1,0:T(8,128)(2,1)S(1)} %get-tuple-element.19.values_ref, bf16[512,128]{1,0:T(8,128)(2,1)S(1)} %get-tuple-element.20.queries_ref, f32[128,512]{1,0:T(8,128)S(1)} %get-tuple-element.21.qf_ref, ...), custom_call_target="tpu_custom_call" | custom-call | flops 1000000000 | bytes 10000000 | tf_op jit(solution)/shard_map/backward/pallas_call | solution.py:502
  22.3 1.8 %collective-permute-start.3 = (f32[128,128]{1,0:T(8,128)S(1)}, f32[128,128]{1,0:T(8,128)S(1)}, u32[]{:S(2)}, u32[]{:S(2)}) collective-permute-start(f32[128,128]{1,0:T(8,128)S(1)} %backward.1.own_ref), channel_id=1, source_target_pairs={{0,8},{8,0},{16,24},{24,16},{1,9},{9,1},{17,25},{25,17},{2,10},{10... | collective-permute-start | bytes 196616 | tf_op jit(solution)/shard_map/ppermute | solution.py:500
  24.1 0.0 collective-permute-done.6
  24.1 0.0 collective-permute-done.5
  24.1 0.2 collective-permute-done.4
  24.4 1.8 %collective-permute-start.7 = (f32[8,128]{1,0:T(8,128)S(1)}, f32[8,128]{1,0:T(8,128)S(1)}, u32[]{:S(2)}, u32[]{:S(2)}) collective-permute-start(f32[8,128]{1,0:T(8,128)S(1)} %add_add_fusion.refs_0_), channel_id=1, source_target_pairs={{0,8},{8,0},{16,24},{24,16},{1,9},{9,1},{17,25},{25,17},{2,10},{10... | collective-permute-start | bytes 12296 | tf_op jit(solution)/shard_map/ppermute | solution.py:500
  26.1 1.9 %collective-permute-done.7.refs_1_ = f32[8,128]{1,0:T(8,128)S(1)} collective-permute-done((f32[8,128]{1,0:T(8,128)S(1)}, f32[8,128]{1,0:T(8,128)S(1)}, u32[]{:S(2)}, u32[]{:S(2)}) %collective-permute-start.7) | collective-permute-done | bytes 4128 | tf_op jit(solution)/shard_map/ppermute | solution.py:500
  28.0 0.0 collective-permute-done.3.other_ref
  28.0 0.7 %join.1 = (f32[2,64,128]{2,1,0:T(8,128)}, f32[2,64,128]{2,1,0:T(8,128)}, f32[1]{0:T(128)}) custom-call(f32[128,128]{1,0:T(8,128)S(1)} %backward.1.own_ref, f32[128,128]{1,0:T(8,128)S(1)} %collective-permute-done.3.other_ref, f32[8,128]{1,0:T(8,128)S(1)} %add_add_fusion.refs_0_, f32[8,128]{1,0:T(8,128)S(1)} %collective-permute-done.7.refs_1_), custom_call_target="tpu_custom_call" | custom-call | tf_op jit(solution)/shard_map/join/pallas_call | solution.py:513
  (1 shorter events, 0.0 us)
Async XLA Ops:
  0.6 13.5 %copy-start.1 = (f32[2,64,128]{2,1,0:T(8,128)S(1)}, f32[2,64,128]{2,1,0:T(8,128)}, u32[]{:S(2)}) copy-start(f32[2,64,128]{2,1,0:T(8,128)} %refs_5_.1) | copy-start | bytes 196612
  0.6 13.5 %copy-start = (f32[2,64,128]{2,1,0:T(8,128)S(1)}, f32[2,64,128]{2,1,0:T(8,128)}, u32[]{:S(2)}) copy-start(f32[2,64,128]{2,1,0:T(8,128)} %refs_4_.1) | copy-start | bytes 196612
  1.9 10.6 %collective-permute-start.1 = (bf16[384,128]{1,0:T(8,128)(2,1)S(1)}, bf16[384,128]{1,0:T(8,128)(2,1)S(1)}, u32[]{:S(2)}, u32[]{:S(2)}) collective-permute-start(bf16[384,128]{1,0:T(8,128)(2,1)S(1)} %get-tuple-element.16.refs_0_), channel_id=1, source_target_pairs={{0,16},{8,24},{16,0},{24,8},{1,17},{9,25},{17,1},{25,9},{2,18},{10... | collective-permute-start | bytes 294920 | tf_op jit(solution)/shard_map/ppermute | solution.py:475
  6.0 6.4 %collective-permute-start.2 = (bf16[384,128]{1,0:T(8,128)(2,1)S(1)}, bf16[384,128]{1,0:T(8,128)(2,1)S(1)}, u32[]{:S(2)}, u32[]{:S(2)}) collective-permute-start(bf16[384,128]{1,0:T(8,128)(2,1)S(1)} %get-tuple-element.17), channel_id=1, source_target_pairs={{0,24},{8,0},{16,8},{24,16},{1,25},{9,1},{17,9},{25,17},{2,26},{10... | collective-permute-start | bytes 294920 | tf_op jit(solution)/shard_map/ppermute | solution.py:475
  7.4 6.8 %collective-permute-start = (bf16[384,128]{1,0:T(8,128)(2,1)S(1)}, bf16[384,128]{1,0:T(8,128)(2,1)S(1)}, u32[]{:S(2)}, u32[]{:S(2)}) collective-permute-start(bf16[384,128]{1,0:T(8,128)(2,1)S(1)} %get-tuple-element.17), channel_id=1, source_target_pairs={{0,8},{8,16},{16,24},{24,0},{1,9},{9,17},{17,25},{25,1},{2,10},{10... | collective-permute-start | bytes 294920 | tf_op jit(solution)/shard_map/ppermute | solution.py:475
  16.9 7.2 %collective-permute-start.6 = (f32[8,128]{1,0:T(8,128)S(1)}, f32[8,128]{1,0:T(8,128)S(1)}, u32[]{:S(2)}, u32[]{:S(2)}) collective-permute-start(f32[8,128]{1,0:T(8,128)S(1)} %get-tuple-element.25), channel_id=1, source_target_pairs={{0,6},{2,0},{4,2},{6,4},{1,7},{3,1},{5,3},{7,5},{8,14},{10,8},{12,... | collective-permute-start | bytes 12296 | tf_op jit(solution)/shard_map/ppermute | solution.py:475
  19.4 4.8 %collective-permute-start.5 = (f32[8,128]{1,0:T(8,128)S(1)}, f32[8,128]{1,0:T(8,128)S(1)}, u32[]{:S(2)}, u32[]{:S(2)}) collective-permute-start(f32[8,128]{1,0:T(8,128)S(1)} %get-tuple-element.25), channel_id=1, source_target_pairs={{0,4},{2,6},{4,0},{6,2},{1,5},{3,7},{5,1},{7,3},{8,12},{10,14},{12... | collective-permute-start | bytes 12296 | tf_op jit(solution)/shard_map/ppermute | solution.py:475
  19.9 4.5 %collective-permute-start.4 = (f32[8,128]{1,0:T(8,128)S(1)}, f32[8,128]{1,0:T(8,128)S(1)}, u32[]{:S(2)}, u32[]{:S(2)}) collective-permute-start(f32[8,128]{1,0:T(8,128)S(1)} %get-tuple-element.25), channel_id=1, source_target_pairs={{0,2},{2,4},{4,6},{6,0},{1,3},{3,5},{5,7},{7,1},{8,10},{10,12},{12... | collective-permute-start | bytes 12296 | tf_op jit(solution)/shard_map/ppermute | solution.py:475
  22.3 5.7 %collective-permute-start.3 = (f32[128,128]{1,0:T(8,128)S(1)}, f32[128,128]{1,0:T(8,128)S(1)}, u32[]{:S(2)}, u32[]{:S(2)}) collective-permute-start(f32[128,128]{1,0:T(8,128)S(1)} %backward.1.own_ref), channel_id=1, source_target_pairs={{0,8},{8,0},{16,24},{24,16},{1,9},{9,1},{17,25},{25,17},{2,10},{10... | collective-permute-start | bytes 196616 | tf_op jit(solution)/shard_map/ppermute | solution.py:500
  24.4 3.6 %collective-permute-start.7 = (f32[8,128]{1,0:T(8,128)S(1)}, f32[8,128]{1,0:T(8,128)S(1)}, u32[]{:S(2)}, u32[]{:S(2)}) collective-permute-start(f32[8,128]{1,0:T(8,128)S(1)} %add_add_fusion.refs_0_), channel_id=1, source_target_pairs={{0,8},{8,0},{16,24},{24,16},{1,9},{9,1},{17,25},{25,17},{2,10},{10... | collective-permute-start | bytes 12296 | tf_op jit(solution)/shard_map/ppermute | solution.py:500

commit v3 on v2

--- a/solution.py
+++ b/solution.py
@@ -14,7 +14,6 @@
 exact = lax.Precision.HIGHEST
 f32, bf16 = jnp.float32, jnp.bfloat16
 PAD = 16
-LIMIT = 8
 SMALL, LARGE = 4 << 20, 24 << 20
 
 
@@ -227,33 +226,66 @@
 
 
 def dot3(a, b):
-    return dot(a[0], b[0]) + (dot(a[0], b[1]) + dot(a[1], b[0]))
+    return dot(jnp.concatenate([a[0], a[1], a[0]], axis=1), jnp.concatenate([b[0], b[0], b[1]], axis=0))
 
 
 def dot_left(a, b):
-    return dot(a[0], b) + dot(a[1], b)
+    return dot(jnp.concatenate(a, axis=1), jnp.concatenate([b, b], axis=0))
 
 
 def dot_right(a, b):
-    return dot(a, b[0]) + dot(a, b[1])
+    return dot(jnp.concatenate([a, a], axis=1), jnp.concatenate(b, axis=0))
 
 
 def iota(shape, axis):
     return lax.broadcasted_iota(jnp.int32, shape, axis)
 
 
-def forward_pass(queries, keys, ext_keys, values_t, ext_aug_t, pair_sum, query_weight, key_weight, block, tokens_total):
+def feature_weights(weights):
+    high, low = split(jnp.concatenate([part for weight in weights for part in (weight, -weight)], axis=0))
+    return jnp.concatenate([high, low], axis=1)
+
+
+def features_of(rows, weights):
+    raised = jnp.exp(dot_t(jnp.concatenate([rows, rows], axis=1), weights))
+    size, half = raised.shape[1], rows.shape[1] // 2
+    same = (iota((size, size), 0) // half == iota((size, size), 1) // half).astype(bf16)
+    return raised / dot_left(split(raised), same)
+
+
+def absorb(piece_rows, source, kv, q, query_weight_ref, key_weight_ref, buffers):
+    keys_ref, values_ref, queries_ref, kf_ref, qn_ref, qt_ref = buffers
+    heads, width = queries_ref.shape[0], queries_ref.shape[2]
+    at = pl.multiple_of(source * piece_rows, piece_rows)
+    here, shifted = pl.ds(at, piece_rows), pl.ds(pl.multiple_of(at + WINDOW, WINDOW), piece_rows)
+    if kv is not None:
+        ref, skip = kv
+        keys = ref[skip * piece_rows : (skip + 1) * piece_rows]
+        keys_ref[shifted] = keys
+        values_ref[shifted] = ref[(skip + 1) * piece_rows : (skip + 2) * piece_rows]
+        found = features_of(keys, feature_weights([key_weight_ref[h] for h in range(heads)]))
+        for h in range(heads):
+            high, low = split(found[:, h * width : (h + 1) * width])
+            kf_ref[h, shifted, :width] = high
+            kf_ref[h, shifted, width:] = low
+    if q is not None:
+        ref, skip = q
+        for h in range(heads):
+            queries = ref[(skip + h) * piece_rows : (skip + h + 1) * piece_rows]
+            queries_ref[h, here] = queries
+            found = features_of(queries, feature_weights([query_weight_ref[h]]))
+            high, low = split(found)
+            qn_ref[h, here, :width] = high
+            qn_ref[h, here, width:] = low
+            high, low = split(found.T)
+            qt_ref[h, :width, here] = high
+            qt_ref[h, width:, here] = low
+
+
+def forward_pass(queries, keys, kf_s, qf_ts, values_t, ext_aug_t, block, tokens_total):
     tokens, width = queries.shape
     blocks = tokens // block
     scale = width ** (-0.5)
-    wq = split(jnp.concatenate([query_weight, -query_weight], axis=0))
-    wk = split(jnp.concatenate([key_weight, -key_weight], axis=0))
-    raised_t = jnp.exp(dot_t(wq[0], queries) + dot_t(wq[1], queries))
-    qf_t = raised_t / dot_right(pair_sum, split(raised_t))
-    raised = jnp.exp(dot_t(ext_keys, wk[0]) + dot_t(ext_keys, wk[1]))
-    kf = raised / dot_left(split(raised), pair_sum)
-    kf = jnp.where(iota(kf.shape, 0) >= WINDOW, kf, 0.0)
-    qf_ts, kf_s = split(qf_t), split(kf)
     tri = iota((block, block), 0) <= iota((block, block), 1)
     near = iota((block + WINDOW, block), 0) > iota((block + WINDOW, block), 1)
     loss = jnp.zeros((1, 1), f32)
@@ -305,18 +337,19 @@
         grad = difference * (2.0 / tokens_total)
         nums.append(grad * (lift * over))
         dens.append(-(lift * over) * jnp.sum(grad * student, axis=0, keepdims=True))
-    return loss, qf_t, kf, nums, dens
+    return loss, nums, dens
 
 
 def cut(pair, at):
     return tuple(part[at] for part in pair)
 
 
-def backward_pass(qf_t, kf, nums, dens, queries, ext_values, ext_keys_t, pair_sum, block):
+def backward_pass(kf_s, qf_s, qf_ts, nums, dens, queries, ext_values, ext_keys_t, pair_sum, block):
     width, tokens = queries.shape[1], queries.shape[0]
     blocks = tokens // block
     tri = iota((block, block), 0) <= iota((block, block), 1)
-    qf_s, kf_ts = split(qf_t.T), split(kf.T)
+    kf, qf_t = joined(kf_s), joined(qf_ts)
+    kf_ts = split(kf.T)
     ext_aug = jnp.concatenate([ext_values, (iota((tokens, width), 1) == 0).astype(bf16)], axis=1)
     states = [None]
     for b in range(blocks - 1):
@@ -355,6 +388,10 @@
     return grad_q[:half] - grad_q[half:], grad_k[:half] - grad_k[half:]
 
 
+def joined(pair):
+    return pair[0].astype(f32) + pair[1].astype(f32)
+
+
 def turned(x):
     eye = (iota((x.shape[1], x.shape[1]), 0) == iota((x.shape[1], x.shape[1]), 1)).astype(bf16)
     return dot_t(eye, x).astype(bf16)
@@ -369,163 +406,186 @@
     return ((iota((features, features), 0) < half) == (iota((features, features), 1) < half)).astype(bf16)
 
 
-def pack_kernel(queries_ref, keys_ref, values_ref, same_ref, other_ref, queries_in, sems):
+def pack_kernel(queries_ref, keys_ref, values_ref, all_ref, keys_values_ref, queries_out_ref, queries_in, sems):
     rows = keys_ref.shape[0]
+    first, second = pl.ds(0, rows), pl.ds(rows, rows)
     copies = [
         pltpu.make_async_copy(queries_ref, queries_in, sems.at[0]),
-        pltpu.make_async_copy(keys_ref, same_ref.at[pl.ds(0, rows)], sems.at[1]),
-        pltpu.make_async_copy(values_ref, same_ref.at[pl.ds(rows, rows)], sems.at[2]),
-        pltpu.make_async_copy(keys_ref, other_ref.at[pl.ds(0, rows)], sems.at[3]),
-        pltpu.make_async_copy(values_ref, other_ref.at[pl.ds(rows, rows)], sems.at[4]),
+        pltpu.make_async_copy(keys_ref, all_ref.at[first], sems.at[1]),
+        pltpu.make_async_copy(values_ref, all_ref.at[second], sems.at[2]),
+        pltpu.make_async_copy(keys_ref, keys_values_ref.at[first], sems.at[3]),
+        pltpu.make_async_copy(values_ref, keys_values_ref.at[second], sems.at[4]),
     ]
     for copy in copies:
         copy.start()
-    odd = lax.rem(lax.axis_index("seq"), 2) == 1
     copies[0].wait()
-    first, second = queries_in[:, 0, :], queries_in[:, 1, :]
-    same_ref[2 * rows :] = jnp.where(odd, second, first)
-    other_ref[2 * rows :] = jnp.where(odd, first, second)
+    for h in range(queries_ref.shape[1]):
+        part = queries_in[:, h, :]
+        all_ref[(2 + h) * rows : (3 + h) * rows] = part
+        queries_out_ref[h * rows : (h + 1) * rows] = part
     for copy in copies[1:]:
         copy.wait()
 
 
-def forward_kernel(shards, rows, *refs):
-    blocks_in = refs[:shards]
-    query_weight_ref, key_weight_ref, loss_ref, keys_ref, values_ref, queries_ref, qf_ref, kf_ref, num_ref, den_ref = refs[shards : shards + 10]
-    qw_ref, kw_ref, sems = refs[shards + 10 :]
-    tokens, width = queries_ref.shape
+def absorb_kernel(rows, parts, fresh, *refs):
+    piece_refs, refs = refs[: len(parts)], refs[len(parts) :]
+    query_weight_ref, key_weight_ref = refs[:2]
+    buffers = refs[2:] if fresh else refs[8:]
+    keys_ref, values_ref, _, kf_ref, _, _ = buffers
+    if fresh:
+        for ref in (keys_ref, values_ref):
+            ref[:WINDOW] = jnp.zeros((WINDOW, ref.shape[1]), bf16)
+        kf_ref[:, :WINDOW] = jnp.zeros((kf_ref.shape[0], WINDOW, kf_ref.shape[2]), bf16)
+    take(rows, parts, piece_refs, query_weight_ref, key_weight_ref, buffers)
+
+
+def take(rows, parts, piece_refs, query_weight_ref, key_weight_ref, buffers):
     place = lax.axis_index("seq")
-    mine = lax.rem(place, 2)
-    copies = []
-    for d in range(shards):
-        source = lax.rem(place + shards - d, shards)
-        at = pl.multiple_of(source * rows, rows)
-        for k, (ref, offset) in enumerate(((keys_ref, WINDOW), (values_ref, WINDOW), (queries_ref, 0))):
-            copies.append(
-                pltpu.make_async_copy(
-                    blocks_in[d].at[pl.ds(k * rows, rows)], ref.at[pl.ds(at + offset, rows)], sems.at[3 * d + k]
-                )
-            )
-    copies.append(pltpu.make_async_copy(query_weight_ref.at[mine], qw_ref, sems.at[3 * shards]))
-    copies.append(pltpu.make_async_copy(key_weight_ref.at[mine], kw_ref, sems.at[3 * shards + 1]))
-    for copy in copies:
-        copy.start()
-    keys_ref[:WINDOW] = jnp.zeros((WINDOW, width), bf16)
-    values_ref[:WINDOW] = jnp.zeros((WINDOW, width), bf16)
-    for copy in copies:
-        copy.wait()
+    for (d, kind, _), ref in zip(parts, piece_refs):
+        kv = (ref, 0) if kind in ("both", "kv") else None
+        q = (ref, 2 if kind == "both" else 0) if kind in ("both", "q") else None
+        absorb(rows, partner(place, d), kv, q, query_weight_ref, key_weight_ref, buffers)
+
+
+def forward_kernel(rows, parts, *refs):
+    piece_refs, refs = refs[: len(parts)], refs[len(parts) :]
+    query_weight_ref, key_weight_ref = refs[:2]
+    keys_ref, values_ref, queries_ref, kf_ref, qn_ref, qt_ref = buffers = refs[8:14]
+    loss_ref, num_ref, den_ref = refs[14:]
+    take(rows, parts, piece_refs, query_weight_ref, key_weight_ref, buffers)
+    heads, tokens, width = queries_ref.shape
     block = block_of(tokens)
-    loss, qf_t, kf, nums, dens = forward_pass(
-        queries_ref[...], keys_ref[WINDOW:], keys_ref[:tokens], turned(values_ref[WINDOW:]),
-        with_ones(turned(values_ref[:tokens])), pair_sums(2 * qw_ref.shape[0]), qw_ref[...], kw_ref[...], block, tokens,
-    )
-    qf_ref[...] = qf_t
-    kf_ref[...] = kf
-    for b in range(tokens // block):
-        at = slice(b * block, (b + 1) * block)
-        num_ref[:, at] = nums[b]
-        den_ref[:, at] = jnp.broadcast_to(dens[b], (8, block))
-    loss_ref[...] = jnp.broadcast_to(loss / tokens, loss_ref.shape)
+    values_t, aug_t = turned(values_ref[WINDOW:]), with_ones(turned(values_ref[:tokens]))
+    total = jnp.zeros((1, 1), f32)
+    for h in range(heads):
+        kf_s = (kf_ref[h, :tokens, :width], kf_ref[h, :tokens, width:])
+        loss, nums, dens = forward_pass(
+            queries_ref[h], keys_ref[WINDOW:], kf_s, (qt_ref[h, :width], qt_ref[h, width:]), values_t, aug_t, block, tokens
+        )
+        total = total + loss
+        for b in range(tokens // block):
+            at = slice(b * block, (b + 1) * block)
+            num_ref[h, :, at] = nums[b]
+            den_ref[h, :, at] = jnp.broadcast_to(dens[b], (8, block))
+    loss_ref[...] = jnp.broadcast_to(total / tokens, loss_ref.shape)
+
+
+def partner(place, d):
+    if d & 1:
+        place = place + 1 - 2 * lax.rem(place, 2)
+    if d & 2:
+        place = lax.rem(place + 2, 4)
+    return place
 
 
 def block_of(tokens):
     return 256 if tokens % 256 == 0 else 128
 
 
-def backward_kernel(keys_ref, values_ref, queries_ref, qf_ref, kf_ref, num_ref, den_ref, grads_ref):
-    tokens = queries_ref.shape[0]
-    half = qf_ref.shape[0] // 2
+def backward_kernel(keys_ref, values_ref, queries_ref, kf_ref, qn_ref, qt_ref, num_ref, den_ref, grad_q_ref, grad_k_ref):
+    heads, tokens, width = queries_ref.shape
     block = block_of(tokens)
     cuts = [slice(b * block, (b + 1) * block) for b in range(tokens // block)]
-    grads_ref[:half], grads_ref[half:] = backward_pass(
-        qf_ref[...], kf_ref[...], [num_ref[:, at] for at in cuts], [den_ref[:1, at] for at in cuts],
-        queries_ref[...], values_ref[:tokens], turned(keys_ref[:tokens]), pair_sums(2 * half), block,
-    )
-
-
-def join_kernel(own_ref, other_ref, *refs):
-    loss_refs = refs[:-3]
-    grad_q_ref, grad_k_ref, loss_ref = refs[-3:]
-    half = grad_q_ref.shape[1]
-    odd = lax.rem(lax.axis_index("seq"), 2) == 1
-    own, other = own_ref[...], other_ref[...]
-    first, second = jnp.where(odd, other, own), jnp.where(odd, own, other)
-    grad_q_ref[0], grad_q_ref[1] = first[:half], second[:half]
-    grad_k_ref[0], grad_k_ref[1] = first[half:], second[half:]
-    loss_ref[0] = sum(ref[0, 0] for ref in loss_refs)
+    keys_t, sums = turned(keys_ref[:tokens]), pair_sums(width)
+    for h in range(heads):
+        grad_q_ref[h], grad_k_ref[h] = backward_pass(
+            (kf_ref[h, :tokens, :width], kf_ref[h, :tokens, width:]), (qn_ref[h, :, :width], qn_ref[h, :, width:]),
+            (qt_ref[h, :width], qt_ref[h, width:]), [num_ref[h, :, at] for at in cuts],
+            [den_ref[h, :1, at] for at in cuts], queries_ref[h], values_ref[:tokens], keys_t, sums, block,
+        )
+
+
+def add_kernel(*refs):
+    refs[-1][0] = sum(ref[0, 0] for ref in refs[:-1])
 
 
 def local_gathered(queries, keys, values, query_weight, key_weight):
-    rows, local_heads, width = queries.shape
+    rows, heads, width = queries.shape
     features = query_weight.shape[1]
     shards, columns = lax.axis_size("seq"), lax.axis_size("head")
     tokens = rows * shards
     vmem = pl.BlockSpec(memory_space=pltpu.VMEM)
     anywhere = pl.BlockSpec(memory_space=pl.ANY)
     shape = jax.ShapeDtypeStruct
-    same, other = pl.pallas_call(
+    own, own_kv, own_q = pl.pallas_call(
         pack_kernel,
-        out_shape=(shape((3 * rows, width), bf16),) * 2,
+        out_shape=(
+            shape(((2 + heads) * rows, width), bf16), shape((2 * rows, width), bf16), shape((heads * rows, width), bf16)
+        ),
         in_specs=[pl.BlockSpec(memory_space=pltpu.HBM)] * 3,
-        out_specs=(vmem,) * 2,
+        out_specs=(vmem,) * 3,
         scratch_shapes=[pltpu.VMEM(queries.shape, bf16), pltpu.SemaphoreType.DMA((5,))],
         compiler_params=pltpu.CompilerParams(vmem_limit_bytes=SMALL),
         name="pack",
     )(*(pltpu.with_memory_space_constraint(x, pltpu.HBM) for x in (queries, keys, values)))
-    turn = lambda x, axis, size, d: lax.ppermute(x, axis, [(i, (i + d) % size) for i in range(size)])
-    pieces = [same] + [turn(other if d % 2 else same, "seq", shards, d) for d in range(1, shards)]
-    loss, *kept = pl.pallas_call(
-        functools.partial(forward_kernel, shards, rows),
-        out_shape=(
-            shape((8, 128), f32),
-            shape((tokens + WINDOW, width), bf16),
-            shape((tokens + WINDOW, width), bf16),
-            shape((tokens, width), bf16),
-            shape((2 * features, tokens), f32),
-            shape((tokens, 2 * features), f32),
-            shape((width, tokens), f32),
-            shape((8, tokens), f32),
-        ),
-        in_specs=[anywhere] * (shards + 2),
-        out_specs=(vmem,) * 8,
-        scratch_shapes=[
-            pltpu.VMEM((features, width), f32),
-            pltpu.VMEM((features, width), f32),
-            pltpu.SemaphoreType.DMA((3 * shards + 2,)),
-        ],
+    swap = lambda x, axis, size, d: lax.ppermute(x, axis, [(i, i ^ d) for i in range(size)])
+    far_kv = swap(own_kv, "seq", shards, 2)
+    far_q = swap(own_q, "seq", shards, 2)
+    near = swap(own, "seq", shards, 1)
+    last_kv = swap(far_kv, "seq", shards, 1)
+    last_q = swap(far_q, "seq", shards, 1)
+    buffers = (
+        shape((tokens + WINDOW, width), bf16),
+        shape((tokens + WINDOW, width), bf16),
+        shape((heads, tokens, width), bf16),
+        shape((heads, tokens + WINDOW, 4 * features), bf16),
+        shape((heads, tokens, 4 * features), bf16),
+        shape((heads, 4 * features, tokens), bf16),
+    )
+
+    def absorbed(parts, held):
+        pieces = [piece for _, _, piece in parts]
+        first = len(pieces) + 2
+        return pl.pallas_call(
+            functools.partial(absorb_kernel, rows, [(d, kind, None) for d, kind, _ in parts], not held),
+            out_shape=buffers,
+            in_specs=[vmem] * (first + len(held)),
+            out_specs=(vmem,) * 6,
+            input_output_aliases={first + i: i for i in range(len(held))},
+            compiler_params=pltpu.CompilerParams(vmem_limit_bytes=SMALL),
+            cost_estimate=pl.CostEstimate(flops=10**8, bytes_accessed=10**6, transcendentals=10**5),
+        )(*pieces, query_weight, key_weight, *held)
+
+    held = absorbed([(0, "both", own)], ())
+    held = absorbed([(2, "kv", far_kv), (2, "q", far_q)], held)
+    held = absorbed([(1, "both", near), (3, "kv", last_kv)], held)
+    *held, loss, num, den = pl.pallas_call(
+        functools.partial(forward_kernel, rows, [(3, "q", None)]),
+        out_shape=buffers + (shape((8, 128), f32), shape((heads, width, tokens), f32), shape((heads, 8, tokens), f32)),
+        in_specs=[vmem] * 9,
+        out_specs=(vmem,) * 9,
+        input_output_aliases={3 + i: i for i in range(6)},
         compiler_params=pltpu.CompilerParams(vmem_limit_bytes=LARGE),
         cost_estimate=pl.CostEstimate(flops=10**9, bytes_accessed=10**7, transcendentals=10**6),
         name="forward",
-    )(*pieces, query_weight, key_weight)
-    swap = lambda x: lax.ppermute(x, "seq", [(i, i ^ 1) for i in range(shards)])
-    loss = sum((turn(loss, "head", columns, d) for d in range(1, columns)), loss)
-    grads = pl.pallas_call(
+    )(last_q, query_weight, key_weight, *held)
+    losses = [loss] + [swap(loss, "head", columns, d) for d in range(1, columns)]
+    grad_query, grad_key = pl.pallas_call(
         backward_kernel,
-        out_shape=shape((2 * features, width), f32),
-        in_specs=[vmem] * 7,
-        out_specs=vmem,
+        out_shape=(shape((heads, features, width), f32),) * 2,
+        in_specs=[vmem] * 8,
+        out_specs=(vmem,) * 2,
         compiler_params=pltpu.CompilerParams(vmem_limit_bytes=LARGE),
         cost_estimate=pl.CostEstimate(flops=10**9, bytes_accessed=10**7, transcendentals=10**6),
         name="backward",
-    )(*kept)
-    other_grads = swap(grads)
-    losses = [loss, swap(loss)]
-    grad_query, grad_key, loss = pl.pallas_call(
-        join_kernel,
-        out_shape=(shape((local_heads, features, width), f32),) * 2 + (shape((1,), f32),),
-        in_specs=[vmem] * 4,
-        out_specs=(vmem, vmem, pl.BlockSpec(memory_space=pltpu.SMEM)),
+    )(*held, num, den)
+    loss = pl.pallas_call(
+        add_kernel,
+        out_shape=shape((1,), f32),
+        in_specs=[vmem] * columns,
+        out_specs=pl.BlockSpec(memory_space=pltpu.SMEM),
         compiler_params=pltpu.CompilerParams(vmem_limit_bytes=SMALL),
         name="join",
-    )(grads, other_grads, *losses)
+    )(*losses)
     return loss, grad_query, grad_key
 
 
 def local(queries, keys, values, query_weight, key_weight):
-    rows, local_heads, width = queries.shape
+    rows, _, width = queries.shape
     shards = lax.axis_size("seq")
-    fits = shards <= LIMIT and shards % 2 == 0 and local_heads == 2 and rows == width == 128
-    if fits and 2 * query_weight.shape[1] == width:
+    columns = lax.axis_size("head")
+    fits = shards == 4 and columns & (columns - 1) == 0 and rows == width == 128 and 2 * query_weight.shape[1] == width
+    if fits:
         return local_gathered(queries, keys, values, query_weight, key_weight)
     return local_general(queries, keys, values, query_weight, key_weight)
 

time: 28.8 us -> 28.7 us (level)
  Pallas kernels: 6.48 us -> 9.89 us
  waiting for transfers between devices: 8.2 us -> 6.18 us
  starting transfers between devices: 13.3 us -> 11.7 us
    pallas_call x4 -> x7, Pallas kernels: 6.48 us -> 9.89 us  [the longest x1 3.74 us: local_gathered(): pl.pallas_call(backward_kernel, out_shape=(shape((heads, features, width)...]
    ppermute x8, waiting for transfers between devices: 8.2 us -> 6.18 us  [local_gathered(): lax.ppermute(x, axis, [(i, i ^ d) for i in range(size)])]
    ppermute x8, starting transfers between devices: 13.3 us -> 11.7 us  [local_gathered(): lax.ppermute(x, axis, [(i, i ^ d) for i in range(size)])]
  transfers between devices with their start and end apart: 8 -> 8, of which waited for: 4 -> 3; matrix products, arithmetic and copies ran while one was open for 0% -> 0% of each run, Pallas kernels for 6% -> 19%
where the time goes in v3:
time: 28.7 us; the launch traced here: 28.5 us
  starting transfers between devices  11.7 us (41%)
  Pallas kernels  9.89 us (34%)
  waiting for transfers between devices  6.18 us (22%)
  between operations  0.7 us (2%)
    ppermute x8, starting transfers between devices, local_gathered(): lax.ppermute(x, axis, [(i, i ^ d) for i in range(size)])  11.7 us
    ppermute x8, waiting for transfers between devices, local_gathered(): lax.ppermute(x, axis, [(i, i ^ d) for i in range(size)])  6.18 us
    pallas_call x1, Pallas kernels, local_gathered(): pl.pallas_call(backward_kernel, out_shape=(shape((heads, features, width)...  3.74 us
    pallas_call x1, Pallas kernels, local_gathered(): pl.pallas_call(functools.partial(forward_kernel, rows, [(3, 'q', None)]),...  2.87 us
    pallas_call x3, Pallas kernels, absorbed(): pl.pallas_call(functools.partial(absorb_kernel, rows, [(d, kind, None) fo...  1.6 us
    pallas_call x1, Pallas kernels, local_gathered(): pl.pallas_call(pack_kernel, out_shape=(shape(((2 + heads) * rows, width),...  1.11 us
  transfers between devices with their start and end apart: 8, of which 3 were waited for; matrix products, arithmetic and copies ran while one was open for 0% of the time, Pallas kernels for 19%

profile of v3, /device:TPU:0, one launch (start us, length us, event | category | flops | bytes accessed | tf_op | source)
XLA Modules:
  0.0 28.5 jit_solution(6466485870596007768)
XLA Ops:
  0.6 0.0 copy-start.1
  0.6 0.0 copy-start
  0.7 1.1 %pack.1 = (bf16[512,128]{1,0:T(8,128)(2,1)S(1)}, bf16[256,128]{1,0:T(8,128)(2,1)S(1)}, bf16[256,128]{1,0:T(8,128)(2,1)S(1)}) custom-call(bf16[128,2,128]{2,1,0:T(2,128)(2,1)} %queries_ref.1, bf16[128,128]{1,0:T(8,128)(2,1)} %keys_ref.1, bf16[128,128]{1,0:T(8,128)(2,1)} %values_ref.1), custom_call_target="tpu_custom_call" | custom-call | tf_op jit(solution)/shard_map/pack/pallas_call | solution.py:510
  1.8 4.1 %collective-permute-start.3 = (bf16[256,128]{1,0:T(8,128)(2,1)S(1)}, bf16[256,128]{1,0:T(8,128)(2,1)S(1)}, u32[]{:S(2)}, u32[]{:S(2)}) collective-permute-start(bf16[256,128]{1,0:T(8,128)(2,1)S(1)} %get-tuple-element.37), channel_id=1, source_target_pairs={{0,16},{8,24},{16,0},{24,8},{1,17},{9,25},{17,1},{25,9},{2,18},{10... | collective-permute-start | bytes 196616 | tf_op jit(solution)/shard_map/ppermute | solution.py:521
  5.9 1.6 %collective-permute-start.2 = (bf16[512,128]{1,0:T(8,128)(2,1)S(1)}, bf16[512,128]{1,0:T(8,128)(2,1)S(1)}, u32[]{:S(2)}, u32[]{:S(2)}) collective-permute-start(bf16[512,128]{1,0:T(8,128)(2,1)S(1)} %get-tuple-element.36.refs_0_), channel_id=1, source_target_pairs={{0,8},{8,0},{16,24},{24,16},{1,9},{9,1},{17,25},{25,17},{2,10},{10... | collective-permute-start | bytes 393224 | tf_op jit(solution)/shard_map/ppermute | solution.py:521
  7.5 0.3 %collective-permute-start = (bf16[256,128]{1,0:T(8,128)(2,1)S(1)}, bf16[256,128]{1,0:T(8,128)(2,1)S(1)}, u32[]{:S(2)}, u32[]{:S(2)}) collective-permute-start(bf16[256,128]{1,0:T(8,128)(2,1)S(1)} %get-tuple-element.35), channel_id=1, source_target_pairs={{0,16},{8,24},{16,0},{24,8},{1,17},{9,25},{17,1},{25,9},{2,18},{10... | collective-permute-start | bytes 196616 | tf_op jit(solution)/shard_map/ppermute | solution.py:521
  7.8 1.1 %collective-permute-done.3.refs_0_ = bf16[256,128]{1,0:T(8,128)(2,1)S(1)} collective-permute-done((bf16[256,128]{1,0:T(8,128)(2,1)S(1)}, bf16[256,128]{1,0:T(8,128)(2,1)S(1)}, u32[]{:S(2)}, u32[]{:S(2)}) %collective-permute-start.3) | collective-permute-done | bytes 65568 | tf_op jit(solution)/shard_map/ppermute | solution.py:521
  9.0 1.8 %collective-permute-start.4 = (bf16[256,128]{1,0:T(8,128)(2,1)S(1)}, bf16[256,128]{1,0:T(8,128)(2,1)S(1)}, u32[]{:S(2)}, u32[]{:S(2)}) collective-permute-start(bf16[256,128]{1,0:T(8,128)(2,1)S(1)} %collective-permute-done.3.refs_0_), channel_id=1, source_target_pairs={{0,8},{8,0},{16,24},{24,16},{1,9},{9,1},{17,25},{25,17},{2,10},{10... | collective-permute-start | bytes 196616 | tf_op jit(solution)/shard_map/ppermute | solution.py:521
  10.8 2.8 %collective-permute-done.refs_1_ = bf16[256,128]{1,0:T(8,128)(2,1)S(1)} collective-permute-done((bf16[256,128]{1,0:T(8,128)(2,1)S(1)}, bf16[256,128]{1,0:T(8,128)(2,1)S(1)}, u32[]{:S(2)}, u32[]{:S(2)}) %collective-permute-start) | collective-permute-done | bytes 65568 | tf_op jit(solution)/shard_map/ppermute | solution.py:521
  13.6 0.4 %collective-permute-start.1 = (bf16[256,128]{1,0:T(8,128)(2,1)S(1)}, bf16[256,128]{1,0:T(8,128)(2,1)S(1)}, u32[]{:S(2)}, u32[]{:S(2)}) collective-permute-start(bf16[256,128]{1,0:T(8,128)(2,1)S(1)} %collective-permute-done.refs_1_), channel_id=1, source_target_pairs={{0,8},{8,0},{16,24},{24,16},{1,9},{9,1},{17,25},{25,17},{2,10},{10... | collective-permute-start | bytes 196616 | tf_op jit(solution)/shard_map/ppermute | solution.py:521
  13.9 0.0 copy-done.1
  13.9 0.0 copy-done
  13.9 0.5 %shard_map.76 = (bf16[576,128]{1,0:T(8,128)(2,1)S(1)}, bf16[576,128]{1,0:T(8,128)(2,1)S(1)}, bf16[2,512,128]{2,1,0:T(8,128)(2,1)S(1)}, bf16[2,576,256]{2,1,0:T(8...) custom-call(bf16[512,128]{1,0:T(8,128)(2,1)S(1)} %get-tuple-element.36.refs_0_, ...), custom_call_target="tpu_custom_call" | custom-call | flops 100000000 | bytes 1000000 | tf_op jit(solution)/shard_map/pallas_call | solution.py:539
  14.5 0.5 %shard_map.77 = (bf16[576,128]{1,0:T(8,128)(2,1)S(1)}, bf16[576,128]{1,0:T(8,128)(2,1)S(1)}, bf16[2,512,128]{2,1,0:T(8,128)(2,1)S(1)}, bf16[2,576,256]{2,1,0:T(8...) custom-call(bf16[256,128]{1,0:T(8,128)(2,1)S(1)} %collective-permute, ...), custom_call_target="tpu_custom_call", output_to_operand_aliasing={{0}: (4, {}), {1}: (5, {}), {2}: (6, {}), {3}: (7, {}), {4}... | custom-call | flops 100000000 | bytes 1000000 | tf_op jit(solution)/shard_map/pallas_call | solution.py:539
  15.0 0.0 collective-permute-done.4.refs_1_
  15.0 0.0 collective-permute-done.2.refs_0_
  15.0 0.5 %shard_map.78 = (bf16[576,128]{1,0:T(8,128)(2,1)S(1)}, bf16[576,128]{1,0:T(8,128)(2,1)S(1)}, bf16[2,512,128]{2,1,0:T(8,128)(2,1)S(1)}, bf16[2,576,256]{2,1,0:T(8...) custom-call(bf16[512,128]{1,0:T(8,128)(2,1)S(1)} %collective-permute, ...), custom_call_target="tpu_custom_call", output_to_operand_aliasing={{0}: (4, {}), {1}: (5, {}), {2}: (6, {}), {3}: (7, {}), {4}... | custom-call | flops 100000000 | bytes 1000000 | tf_op jit(solution)/shard_map/pallas_call | solution.py:539
  15.6 2.2 %collective-permute-done.1.refs_0_ = bf16[256,128]{1,0:T(8,128)(2,1)S(1)} collective-permute-done((bf16[256,128]{1,0:T(8,128)(2,1)S(1)}, bf16[256,128]{1,0:T(8,128)(2,1)S(1)}, u32[]{:S(2)}, u32[]{:S(2)}) %collective-permute-start.1) | collective-permute-done | bytes 65568 | tf_op jit(solution)/shard_map/ppermute | solution.py:521
  17.8 2.9 %forward.1 = (bf16[576,128]{1,0:T(8,128)(2,1)S(1)}, bf16[576,128]{1,0:T(8,128)(2,1)S(1)}, bf16[2,512,128]{2,1,0:T(8,128)(2,1)S(1)}, bf16[2,576,256]{2,1,0:T(8,12...) custom-call(bf16[256,128]{1,0:T(8,128)(2,1)S(1)} %collective-permute, ...), custom_call_target="tpu_custom_call", output_to_operand_aliasing={{0}: (3, {}), {1}: (4, {}), {2}: (5, {}), {3}: (6, {}), {4}... | custom-call | flops 1000000000 | bytes 10000000 | tf_op jit(solution)/shard_map/forward/pallas_call | solution.py:552
  20.7 2.5 %collective-permute-start.7 = (f32[8,128]{1,0:T(8,128)S(1)}, f32[8,128]{1,0:T(8,128)S(1)}, u32[]{:S(2)}, u32[]{:S(2)}) collective-permute-start(f32[8,128]{1,0:T(8,128)S(1)} %get-tuple-element.56.refs_0_), channel_id=1, source_target_pairs={{0,6},{2,4},{4,2},{6,0},{1,7},{3,5},{5,3},{7,1},{8,14},{10,12},{12... | collective-permute-start | bytes 12296 | tf_op jit(solution)/shard_map/ppermute | solution.py:521
  23.1 0.5 %collective-permute-start.6 = (f32[8,128]{1,0:T(8,128)S(1)}, f32[8,128]{1,0:T(8,128)S(1)}, u32[]{:S(2)}, u32[]{:S(2)}) collective-permute-start(f32[8,128]{1,0:T(8,128)S(1)} %get-tuple-element.56.refs_0_), channel_id=1, source_target_pairs={{0,4},{2,6},{4,0},{6,2},{1,5},{3,7},{5,1},{7,3},{8,12},{10,14},{12... | collective-permute-start | bytes 12296 | tf_op jit(solution)/shard_map/ppermute | solution.py:521
  23.7 0.5 %collective-permute-start.5 = (f32[8,128]{1,0:T(8,128)S(1)}, f32[8,128]{1,0:T(8,128)S(1)}, u32[]{:S(2)}, u32[]{:S(2)}) collective-permute-start(f32[8,128]{1,0:T(8,128)S(1)} %get-tuple-element.56.refs_0_), channel_id=1, source_target_pairs={{0,2},{2,0},{4,6},{6,4},{1,3},{3,1},{5,7},{7,5},{8,10},{10,8},{12,... | collective-permute-start | bytes 12296 | tf_op jit(solution)/shard_map/ppermute | solution.py:521
  24.2 3.7 %backward.1 = (f32[2,64,128]{2,1,0:T(8,128)}, f32[2,64,128]{2,1,0:T(8,128)}) custom-call(bf16[576,128]{1,0:T(8,128)(2,1)S(1)} %get-tuple-element.57.keys_ref, bf16[576,128]{1,0:T(8,128)(2,1)S(1)} %get-tuple-element.58.values_ref, bf16[2,512,128]{2,1,0:T(8,128)(2,1)S(1)} %get-tuple-element.59.queries_ref, bf16[2,576,256]{2,1,0:T(8,128)(2,1)S(1)} %get-tuple-element.60.kf_ref, ...), custom_call_target="tpu_custom_call" | custom-call | flops 1000000000 | bytes 10000000 | tf_op jit(solution)/shard_map/backward/pallas_call | solution.py:563
  27.9 0.0 collective-permute-done.7.refs_3_
  27.9 0.0 collective-permute-done.6.refs_2_
  27.9 0.0 collective-permute-done.5.refs_1_
  27.9 0.6 %join.1 = f32[1]{0:T(128)} custom-call(f32[8,128]{1,0:T(8,128)S(1)} %get-tuple-element.56.refs_0_, f32[8,128]{1,0:T(8,128)S(1)} %collective-permute-done.5.refs_1_, f32[8,128]{1,0:T(8,128)S(1)} %collective-permute-done.6.refs_2_, f32[8,128]{1,0:T(8,128)S(1)} %collective-permute-done.7.refs_3_), custom_call_target="tpu_custom_call" | custom-call | tf_op jit(solution)/shard_map/join/pallas_call | solution.py:572
Async XLA Ops:
  0.6 13.3 %copy-start.1 = (f32[2,64,128]{2,1,0:T(8,128)S(1)}, f32[2,64,128]{2,1,0:T(8,128)}, u32[]{:S(2)}) copy-start(f32[2,64,128]{2,1,0:T(8,128)} %refs_2_.7) | copy-start | bytes 196612
  0.6 13.3 %copy-start = (f32[2,64,128]{2,1,0:T(8,128)S(1)}, f32[2,64,128]{2,1,0:T(8,128)}, u32[]{:S(2)}) copy-start(f32[2,64,128]{2,1,0:T(8,128)} %refs_1_.3) | copy-start | bytes 196612
  1.8 7.2 %collective-permute-start.3 = (bf16[256,128]{1,0:T(8,128)(2,1)S(1)}, bf16[256,128]{1,0:T(8,128)(2,1)S(1)}, u32[]{:S(2)}, u32[]{:S(2)}) collective-permute-start(bf16[256,128]{1,0:T(8,128)(2,1)S(1)} %get-tuple-element.37), channel_id=1, source_target_pairs={{0,16},{8,24},{16,0},{24,8},{1,17},{9,25},{17,1},{25,9},{2,18},{10... | collective-permute-start | bytes 196616 | tf_op jit(solution)/shard_map/ppermute | solution.py:521
  5.9 9.1 %collective-permute-start.2 = (bf16[512,128]{1,0:T(8,128)(2,1)S(1)}, bf16[512,128]{1,0:T(8,128)(2,1)S(1)}, u32[]{:S(2)}, u32[]{:S(2)}) collective-permute-start(bf16[512,128]{1,0:T(8,128)(2,1)S(1)} %get-tuple-element.36.refs_0_), channel_id=1, source_target_pairs={{0,8},{8,0},{16,24},{24,16},{1,9},{9,1},{17,25},{25,17},{2,10},{10... | collective-permute-start | bytes 393224 | tf_op jit(solution)/shard_map/ppermute | solution.py:521
  7.5 6.1 %collective-permute-start = (bf16[256,128]{1,0:T(8,128)(2,1)S(1)}, bf16[256,128]{1,0:T(8,128)(2,1)S(1)}, u32[]{:S(2)}, u32[]{:S(2)}) collective-permute-start(bf16[256,128]{1,0:T(8,128)(2,1)S(1)} %get-tuple-element.35), channel_id=1, source_target_pairs={{0,16},{8,24},{16,0},{24,8},{1,17},{9,25},{17,1},{25,9},{2,18},{10... | collective-permute-start | bytes 196616 | tf_op jit(solution)/shard_map/ppermute | solution.py:521
  9.0 6.1 %collective-permute-start.4 = (bf16[256,128]{1,0:T(8,128)(2,1)S(1)}, bf16[256,128]{1,0:T(8,128)(2,1)S(1)}, u32[]{:S(2)}, u32[]{:S(2)}) collective-permute-start(bf16[256,128]{1,0:T(8,128)(2,1)S(1)} %collective-permute-done.3.refs_0_), channel_id=1, source_target_pairs={{0,8},{8,0},{16,24},{24,16},{1,9},{9,1},{17,25},{25,17},{2,10},{10... | collective-permute-start | bytes 196616 | tf_op jit(solution)/shard_map/ppermute | solution.py:521
  13.6 4.3 %collective-permute-start.1 = (bf16[256,128]{1,0:T(8,128)(2,1)S(1)}, bf16[256,128]{1,0:T(8,128)(2,1)S(1)}, u32[]{:S(2)}, u32[]{:S(2)}) collective-permute-start(bf16[256,128]{1,0:T(8,128)(2,1)S(1)} %collective-permute-done.refs_1_), channel_id=1, source_target_pairs={{0,8},{8,0},{16,24},{24,16},{1,9},{9,1},{17,25},{25,17},{2,10},{10... | collective-permute-start | bytes 196616 | tf_op jit(solution)/shard_map/ppermute | solution.py:521
  20.7 7.2 %collective-permute-start.7 = (f32[8,128]{1,0:T(8,128)S(1)}, f32[8,128]{1,0:T(8,128)S(1)}, u32[]{:S(2)}, u32[]{:S(2)}) collective-permute-start(f32[8,128]{1,0:T(8,128)S(1)} %get-tuple-element.56.refs_0_), channel_id=1, source_target_pairs={{0,6},{2,4},{4,2},{6,0},{1,7},{3,5},{5,3},{7,1},{8,14},{10,12},{12... | collective-permute-start | bytes 12296 | tf_op jit(solution)/shard_map/ppermute | solution.py:521
  23.1 4.8 %collective-permute-start.6 = (f32[8,128]{1,0:T(8,128)S(1)}, f32[8,128]{1,0:T(8,128)S(1)}, u32[]{:S(2)}, u32[]{:S(2)}) collective-permute-start(f32[8,128]{1,0:T(8,128)S(1)} %get-tuple-element.56.refs_0_), channel_id=1, source_target_pairs={{0,4},{2,6},{4,0},{6,2},{1,5},{3,7},{5,1},{7,3},{8,12},{10,14},{12... | collective-permute-start | bytes 12296 | tf_op jit(solution)/shard_map/ppermute | solution.py:521
  23.7 4.3 %collective-permute-start.5 = (f32[8,128]{1,0:T(8,128)S(1)}, f32[8,128]{1,0:T(8,128)S(1)}, u32[]{:S(2)}, u32[]{:S(2)}) collective-permute-start(f32[8,128]{1,0:T(8,128)S(1)} %get-tuple-element.56.refs_0_), channel_id=1, source_target_pairs={{0,2},{2,0},{4,6},{6,4},{1,3},{3,1},{5,7},{7,5},{8,10},{10,8},{12,... | collective-permute-start | bytes 12296 | tf_op jit(solution)/shard_map/ppermute | solution.py:521
